TPU v7x, 256 devices: a whole 4x4x8 slice. The times are simulated.
256 devices in a mesh: segment: 8 (over x, core), dp: 32 (over z, y).
Axes of the slice: x: 4, y: 4, z: 8, core: 2. Of those that a mesh axis runs over, the one named last changes fastest.
Arguments:
- images: bfloat16 [32, 14, 14, 384], P('dp'), may hold values from -6 to 6
- cotangent: bfloat16 [2, 32, 14, 14, 384], P(None, 'dp'), may hold values from -6 to 6
- picks: int32 [2, 16], P(None, 'segment'), may hold values from 0 to 47
- section_sizes: int32 [8], P('segment'), may hold values from 1 to 2, 12 in all
- kernels: bfloat16 [16, 48, 25, 384], P('segment'), may hold values from -1.1953125 to 1.1953125
- weights: bfloat16 [16, 48, 384, 384], P('segment', None, 'dp'), may hold values from -0.15625 to 0.15625
- first_moment: float32 [16, 48, 384, 384], P('segment', None, 'dp'), may hold values from -0.006 to 0.006
- second_moment: float32 [16, 48, 384, 384], P('segment', None, 'dp'), may hold values from 1e-08 to 1e-07
Outputs:
- new_weights: bfloat16 [2, 16, 384, 384], P(None, 'segment', 'dp')
- new_first: float32 [2, 16, 384, 384], P(None, 'segment', 'dp')
- new_second: float32 [2, 16, 384, 384], P(None, 'segment', 'dp')
Inputs may be any that keep to these rules, and one draw needn't show every extreme that they name: `section_sizes`: the counts sum to 12, and one of them equals 2.
All inputs are finite; a program needn't handle non-finite values. No bound on the sum of `section_sizes` on one device may be relied on, other than what follows from the above.
Results may differ from a plain program's by a relative error of at most 0.03.
Values may be sent and summed in bfloat16 or wider, within the bound.
No kernel may reach another device: no remote copies, remote signals or barrier semaphores. Data moves between devices by JAX's collectives and lax.ppermute only.
A program may use at most 128 MiB of HBM per device.

v0:
```python
import jax
import jax.numpy as jnp
from jax import lax
from jax.sharding import PartitionSpec as P

first_decay = 0.9
second_decay = 0.999
learn_rate = 0.01
adam_epsilon = 1e-08
first_bias = 1.0 - 0.9**10
second_bias = 1.0 - 0.999**10


def from_behind(x, axis, by):
    length = lax.axis_size(axis)
    pairs = [(i, i + by) for i in range(length) if 0 <= i + by < length]
    return lax.ppermute(x, axis, pairs)


def spatial(field, kernel, flipped):
    side = field.shape[1]
    padded = jnp.pad(field, ((0, 0), (2, 2), (2, 2), (0, 0)))
    total = jnp.zeros(field.shape, jnp.float32)
    for row_tap in range(5):
        for col_tap in range(5):
            row_start = 4 - row_tap if flipped else row_tap
            col_start = 4 - col_tap if flipped else col_tap
            window = padded[:, row_start : row_start + side, col_start : col_start + side, :]
            total = total + kernel[row_tap * 5 + col_tap].astype(jnp.float32) * window
    return total


def block_forward(inputs, kernel, weight):
    width = inputs.shape[-1]
    mixed = spatial(inputs.astype(jnp.float32), kernel, False)
    hidden = jax.nn.silu(mixed).astype(jnp.bfloat16)
    update = jnp.dot(hidden.reshape(-1, width), weight, preferred_element_type=jnp.float32)
    return (inputs.astype(jnp.float32) + update.reshape(inputs.shape)).astype(jnp.bfloat16)


def block_backward(inputs, upstream, kernel, weight):
    width = inputs.shape[-1]
    mixed = spatial(inputs.astype(jnp.float32), kernel, False)
    hidden = jax.nn.silu(mixed).astype(jnp.bfloat16)
    flat_up = upstream.reshape(-1, width)
    back_hidden = lax.dot_general(
        flat_up, weight, (((1,), (1,)), ((), ())), preferred_element_type=jnp.float32
    )
    back_hidden = back_hidden.reshape(inputs.shape)
    sigma = jax.nn.sigmoid(mixed)
    back_mixed = back_hidden * sigma * (1.0 + mixed * (1.0 - sigma))
    back_inputs = (upstream.astype(jnp.float32) + spatial(back_mixed, kernel, True)).astype(
        jnp.bfloat16
    )
    return (back_inputs, hidden)


def segment_forward(start, kernel_list, net_weights, active_count):
    current = start
    for slot_index in range(len(kernel_list)):
        current = lax.cond(
            slot_index < active_count,
            lambda value: block_forward(value, kernel_list[slot_index], net_weights[slot_index]),
            lambda value: value,
            current,
        )
    return current


def segment_backward(start, upstream, kernel_list, net_weights, active_count):
    slot_total = len(kernel_list)
    stored = []
    current = start
    for slot_index in range(slot_total):
        stored.append(current)
        if slot_index + 1 < slot_total:
            current = lax.cond(
                slot_index < active_count,
                lambda value: block_forward(
                    value, kernel_list[slot_index], net_weights[slot_index]
                ),
                lambda value: value,
                current,
            )
    hiddens = [None] * slot_total
    uppers = [None] * slot_total
    for slot_index in reversed(range(slot_total)):
        uppers[slot_index] = upstream

        def taken(pair):
            return block_backward(
                pair[0], pair[1], kernel_list[slot_index], net_weights[slot_index]
            )

        def skipped(pair):
            return (pair[1], jnp.zeros_like(pair[0]))

        upstream, hidden = lax.cond(
            slot_index < active_count, taken, skipped, (stored[slot_index], upstream)
        )
        hiddens[slot_index] = hidden
    return (upstream, jnp.stack(hiddens), jnp.stack(uppers))


def saved_term(saved_hidden, saved_upper, slot_total, width):
    hidden_flat = jnp.stack(saved_hidden, axis=1).reshape(slot_total * 2, -1, width)
    upper_flat = jnp.stack(saved_upper, axis=1).reshape(slot_total * 2, -1, width)

    def grad_term(start, length):
        return jnp.einsum(
            "srk,srd->ksd", hidden_flat, upper_flat, preferred_element_type=jnp.float32
        )

    return grad_term


def body(images, cotangent, picks, section_sizes, kernels, weights, first_moment, second_moment):
    segments = lax.axis_size("segment")
    place = lax.axis_index("segment")
    slot_total = kernels.shape[0]
    active_count = section_sizes[0]
    width = images.shape[-1]
    rows_here = weights.shape[2]
    total_rows = images.shape[0] * images.shape[1] * images.shape[2] * lax.axis_size("dp")
    chosen_kernels = [
        [
            lax.dynamic_index_in_dim(
                kernels[slot_index], picks[subnet, slot_index], 0, keepdims=False
            )
            for slot_index in range(slot_total)
        ]
        for subnet in range(2)
    ]

    def pick_rows(table):
        return jnp.stack(
            [
                jnp.stack(
                    [
                        lax.dynamic_index_in_dim(
                            table[slot_index], picks[subnet, slot_index], 0, keepdims=False
                        )
                        for subnet in range(2)
                    ]
                )
                for slot_index in range(slot_total)
            ]
        )

    weight_rows = pick_rows(weights)
    first_rows = pick_rows(first_moment)
    second_rows = pick_rows(second_moment)
    gathered = lax.all_gather(weight_rows, "dp", axis=2, tiled=True)
    empty_store = jnp.zeros((slot_total,) + images.shape, jnp.bfloat16)

    def forward_for(subnet):

        def forward_run(value):
            return segment_forward(value, chosen_kernels[subnet], gathered[:, subnet], active_count)

        return forward_run

    def backward_for(subnet, segment_input):

        def backward_run(state):
            return segment_backward(
                segment_input, state[0], chosen_kernels[subnet], gathered[:, subnet], active_count
            )

        return backward_run

    def unchanged(state):
        return state

    saved_hidden = [None, None]
    saved_upper = [None, None]
    segment_inputs = [None, None]
    for subnet in range(2):
        current = images
        segment_input = images
        for step in range(segments):
            turn = place == step
            segment_input = jnp.where(turn, current, segment_input)
            if step + 1 < segments:
                current = lax.cond(turn, forward_for(subnet), unchanged, current)
                current = from_behind(current, "segment", 1)
        segment_inputs[subnet] = segment_input
    for subnet in range(2):
        state = (cotangent[subnet], empty_store, empty_store)
        for step in range(segments):
            turn = place == segments - 1 - step
            state = lax.cond(turn, backward_for(subnet, segment_inputs[subnet]), unchanged, state)
            if step + 1 < segments:
                moved = from_behind(state[0], "segment", -1)
                state = (moved, state[1], state[2])
        saved_hidden[subnet] = state[1]
        saved_upper[subnet] = state[2]
    grad_term = saved_term(saved_hidden, saved_upper, slot_total, width)
    summed = lax.psum_scatter(
        grad_term(jnp.int32(0), rows_here * lax.axis_size("dp")).astype(jnp.bfloat16),
        "dp",
        scatter_dimension=0,
        tiled=True,
    ).astype(jnp.float32)
    summed = summed.reshape(rows_here, slot_total, 2, width)
    out_weights, out_first, out_second = ([], [], [])
    for subnet in range(2):
        row_w, row_m, row_v = ([], [], [])
        for slot_index in range(slot_total):
            own = summed[:, slot_index, subnet]
            other = summed[:, slot_index, 1 - subnet]
            same_pick = picks[subnet, slot_index] == picks[1 - subnet, slot_index]
            grad = (own + jnp.where(same_pick, other, jnp.zeros_like(other))) / total_rows
            weight = weight_rows[slot_index, subnet]
            moment_one = first_rows[slot_index, subnet]
            moment_two = second_rows[slot_index, subnet]
            next_one = first_decay * moment_one + (1.0 - first_decay) * grad
            next_two = second_decay * moment_two + (1.0 - second_decay) * grad * grad
            next_weight = (
                weight.astype(jnp.float32)
                - learn_rate
                * (next_one / first_bias)
                / (jnp.sqrt(next_two / second_bias) + adam_epsilon)
            ).astype(jnp.bfloat16)
            live = slot_index < active_count
            row_w.append(jnp.where(live, next_weight, weight))
            row_m.append(jnp.where(live, next_one, moment_one))
            row_v.append(jnp.where(live, next_two, moment_two))
        out_weights.append(jnp.stack(row_w))
        out_first.append(jnp.stack(row_m))
        out_second.append(jnp.stack(row_v))
    return (jnp.stack(out_weights), jnp.stack(out_first), jnp.stack(out_second))


def solution(mesh):
    return jax.shard_map(
        body,
        mesh=mesh,
        in_specs=(
            P("dp", None, None, None),
            P(None, "dp", None, None, None),
            P(None, "segment"),
            P("segment"),
            P("segment", None, None, None),
            P("segment", None, "dp", None),
            P("segment", None, "dp", None),
            P("segment", None, "dp", None),
        ),
        out_specs=(
            P(None, "segment", "dp", None),
            P(None, "segment", "dp", None),
            P(None, "segment", "dp", None),
        ),
        check_vma=False,
    )
```

profile of v0, /device:TPU:2, one launch (start us, length us, event | category | flops | bytes accessed | tf_op | source)
XLA Modules:
  0.0 469.9 jit_solution(5156747134112352407)
XLA Ops:
  20.2 77.7 %all-gather.2.cloned.1.call-done = bf16[2,2,384,384]{3,1,0,2:T(2,128)(2,1)} async-done(((bf16[2,2,12,384]{3,1,0,2:T(2,128)(2,1)}), bf16[2,2,384,384]{3,1,0,2:T(2,128)(2,1)}) %all-gather.2.cloned.1.call-update) | async-done | bytes 1179664 | tf_op jit(solution)/shard_map/all_gather | solution.py:153
  101.2 3.5 collective-permute-start.14
  108.2 10.2 %conditional.122 = (bf16[1,14,14,384]{3,2,1,0:T(8,128)(2,1)}) conditional(s32[]{:T(128)} %convert_element_type.21000, bf16[1,14,14,384]{3,2,1,0:T(8,128)(2,1)S(1)} %collective-permute-done.14, (s32[]{:T(128)}, bf16[2,2,384,384]{3,1,0,2:T(2,128)(2,1)}, bf16[1,14,14,384]{3,2,1,0:T(8,128)(2,1)S(1)}, bf16[25,384]{1,0:T(8,128)(2,1)S(1)}, ...), branch_computations={%region_112.113_spmd, %region_113.118_spmd} | conditional | flops 124204800 | bytes 6926940 | solution.py:185
  118.3 3.4 collective-permute-start.15
  121.8 8.1 %conditional.108 = (bf16[1,14,14,384]{3,2,1,0:T(8,128)(2,1)}) conditional(s32[]{:T(128)} %convert_element_type.21001, bf16[1,14,14,384]{3,2,1,0:T(8,128)(2,1)S(1)} %collective-permute-done.1, (s32[]{:T(128)}, bf16[2,2,384,384]{3,1,0,2:T(2,128)(2,1)}, bf16[1,14,14,384]{3,2,1,0:T(8,128)(2,1)S(1)}, bf16[25,384]{1,0:T(8,128)(2,1)S(1)}, ...), branch_computations={%region_12.13_spmd, %region_13.18_spmd} | conditional | flops 124204800 | bytes 6926940 | solution.py:185
  126.8 3.1 conditional.5
  133.0 8.1 %conditional.123 = (bf16[1,14,14,384]{3,2,1,0:T(8,128)(2,1)}) conditional(s32[]{:T(128)} %convert_element_type.21001, bf16[1,14,14,384]{3,2,1,0:T(8,128)(2,1)S(1)} %collective-permute-done.15, (s32[]{:T(128)}, bf16[2,2,384,384]{3,1,0,2:T(2,128)(2,1)}, bf16[1,14,14,384]{3,2,1,0:T(8,128)(2,1)S(1)}, bf16[25,384]{1,0:T(8,128)(2,1)S(1)}, ...), branch_computations={%region_118.119_spmd, %region_119.124_spmd} | conditional | flops 124204800 | bytes 6926940 | solution.py:185
  138.0 3.1 conditional.43
  161.0 9.1 %collective-permute-start.5 = (bf16[1,14,14,384]{3,2,1,0:T(8,128)(2,1)}, bf16[1,14,14,384]{3,2,1,0:T(8,128)(2,1)}, u32[]{:S(2)}, u32[]{:S(2)}) collective-permute-start(bf16[1,14,14,384]{3,2,1,0:T(8,128)(2,1)} %get-tuple-element.4681), channel_id=1, source_target_pairs={{0,32},{32,64},{64,96},{96,128},{128,160},{160,192},{192,224},{1,3... | collective-permute-start | bytes 451592 | tf_op jit(solution)/shard_map/ppermute | solution.py:17
  174.9 3.3 collective-permute-start.6
  181.7 5.8 %collective-permute-start.20 = (bf16[1,14,14,384]{3,2,1,0:T(8,128)(2,1)}, bf16[1,14,14,384]{3,2,1,0:T(8,128)(2,1)}, u32[]{:S(2)}, u32[]{:S(2)}) collective-permute-start(bf16[1,14,14,384]{3,2,1,0:T(8,128)(2,1)} %get-tuple-element.4690), channel_id=1, source_target_pairs={{0,32},{32,64},{64,96},{96,128},{128,160},{160,192},{192,224},{1,3... | collective-permute-start | bytes 451592 | tf_op jit(solution)/shard_map/ppermute | solution.py:17
  195.4 3.6 conditional.114
  204.1 3.5 conditional.115
  212.8 3.7 conditional.116
  221.6 3.5 conditional.117
  229.7 26.7 %collective-permute-done.11 = bf16[1,14,14,384]{3,2,1,0:T(8,128)(2,1)S(1)} collective-permute-done((bf16[1,14,14,384]{3,2,1,0:T(8,128)(2,1)}, bf16[1,14,14,384]{3,2,1,0:T(8,128)(2,1)S(1)}, u32[]{:S(2)}, u32[]{:S(2)}) %collective-permute-start.11) | collective-permute-done | bytes 150560 | tf_op jit(solution)/shard_map/ppermute | solution.py:17
  256.3 11.0 %conditional.118 = (bf16[1,14,14,384]{3,2,1,0:T(8,128)(2,1)}, bf16[2,1,14,14,384]{4,3,2,1,0:T(8,128)(2,1)}, bf16[2,1,14,14,384]{4,3,2,1,0:T(8,128)(2,1)}) conditional(s32[]{:T(128)} %convert_element_type.21001, (bf16[1,14,14,384]{3,2,1,0:T(8,128)(2,1)S(1)}, bf16[2,1,14,14,384]{4,3,2,1,0:T(8,128)(2,1)}, ...), branch_computations={%region_82.83_spmd, %region_83.90_spmd} | conditional | flops 195338880 | bytes 19556360 | solution.py:192
  259.4 3.7 conditional.30
  263.2 2.9 conditional.31
  269.2 9.9 %conditional.133 = (bf16[1,14,14,384]{3,2,1,0:T(8,128)(2,1)}, bf16[2,1,14,14,384]{4,3,2,1,0:T(8,128)(2,1)S(1)}, bf16[2,1,14,14,384]{4,3,2,1,0:T(8,128)(2,1)S(1)}) conditional(s32[]{:T(128)} %convert_element_type.21001, (bf16[1,14,14,384]{3,2,1,0:T(8,128)(2,1)S(1)}, bf16[2,1,14,14,384]{4,3,2,1,0:T(8,128)(2,1)S(1)}, ...), branch_computations={%region_188.189_spmd, %region_189.196_spmd} | conditional | flops 195338880 | bytes 19556360 | solution.py:192
  272.3 3.7 conditional.68
  282.1 5.2 %collective-permute-start.13 = (bf16[1,14,14,384]{3,2,1,0:T(8,128)(2,1)}, bf16[1,14,14,384]{3,2,1,0:T(8,128)(2,1)S(1)}, u32[]{:S(2)}, u32[]{:S(2)}) collective-permute-start(bf16[1,14,14,384]{3,2,1,0:T(8,128)(2,1)} %get-tuple-element.1813), channel_id=1, source_target_pairs={{32,0},{64,32},{96,64},{128,96},{160,128},{192,160},{224,192},{33,... | collective-permute-start | bytes 451592 | tf_op jit(solution)/shard_map/ppermute | solution.py:17
  288.0 11.1 %collective-permute-start.27 = (bf16[1,14,14,384]{3,2,1,0:T(8,128)(2,1)}, bf16[1,14,14,384]{3,2,1,0:T(8,128)(2,1)S(1)}, u32[]{:S(2)}, u32[]{:S(2)}) collective-permute-start(bf16[1,14,14,384]{3,2,1,0:T(8,128)(2,1)} %get-tuple-element.1835), channel_id=1, source_target_pairs={{32,0},{64,32},{96,64},{128,96},{160,128},{192,160},{224,192},{33,... | collective-permute-start | bytes 451592 | tf_op jit(solution)/shard_map/ppermute | solution.py:17
  317.0 142.7 %all-reduce.109.cloned.1.call-done = bf16[384,4,384]{2,1,0:T(4,128)(2,1)} async-done(((bf16[384,4,384]{2,1,0:T(4,128)(2,1)}), bf16[384,4,384]{2,1,0:T(4,128)(2,1)}) %all-reduce.109.cloned.1.call-update) | async-done | bytes 1179664
  (264 shorter events, 153.2 us)
Async XLA Ops:
  7.2 90.7 %all-gather.2.cloned.1.call-start = ((), (), s32[]{:S(2)}) async-start(), calls=%async_computation | async-start | bytes 1216512 | tf_op jit(solution)/shard_map/all_gather | solution.py:153
  18.2 441.5 %all-reduce.109.cloned.1.call-start = ((), (), s32[]{:S(2)}) async-start(), calls=%async_computation.1 | async-start | bytes 2359296
  98.6 6.9 %collective-permute-start = (bf16[1,14,14,384]{3,2,1,0:T(8,128)(2,1)}, bf16[1,14,14,384]{3,2,1,0:T(8,128)(2,1)S(1)}, u32[]{:S(2)}, u32[]{:S(2)}) collective-permute-start(bf16[1,14,14,384]{3,2,1,0:T(8,128)(2,1)} %get-tuple-element.4676), channel_id=1, source_target_pairs={{0,32},{32,64},{64,96},{96,128},{128,160},{160,192},{192,224},{1,3... | collective-permute-start | bytes 451592 | tf_op jit(solution)/shard_map/ppermute | solution.py:17
  106.2 15.6 %collective-permute-start.1 = (bf16[1,14,14,384]{3,2,1,0:T(8,128)(2,1)}, bf16[1,14,14,384]{3,2,1,0:T(8,128)(2,1)S(1)}, u32[]{:S(2)}, u32[]{:S(2)}) collective-permute-start(bf16[1,14,14,384]{3,2,1,0:T(8,128)(2,1)} %get-tuple-element.4677), channel_id=1, source_target_pairs={{0,32},{32,64},{64,96},{96,128},{128,160},{160,192},{192,224},{1,3... | collective-permute-start | bytes 451592 | tf_op jit(solution)/shard_map/ppermute | solution.py:17
  118.3 14.7 %collective-permute-start.15 = (bf16[1,14,14,384]{3,2,1,0:T(8,128)(2,1)}, bf16[1,14,14,384]{3,2,1,0:T(8,128)(2,1)S(1)}, u32[]{:S(2)}, u32[]{:S(2)}) collective-permute-start(bf16[1,14,14,384]{3,2,1,0:T(8,128)(2,1)} %get-tuple-element.4685), channel_id=1, source_target_pairs={{0,32},{32,64},{64,96},{96,128},{128,160},{160,192},{192,224},{1,3... | collective-permute-start | bytes 451592 | tf_op jit(solution)/shard_map/ppermute | solution.py:17
  129.8 13.2 %collective-permute-start.2 = (bf16[1,14,14,384]{3,2,1,0:T(8,128)(2,1)}, bf16[1,14,14,384]{3,2,1,0:T(8,128)(2,1)S(1)}, u32[]{:S(2)}, u32[]{:S(2)}) collective-permute-start(bf16[1,14,14,384]{3,2,1,0:T(8,128)(2,1)} %get-tuple-element.4678), channel_id=1, source_target_pairs={{0,32},{32,64},{64,96},{96,128},{128,160},{160,192},{192,224},{1,3... | collective-permute-start | bytes 451592 | tf_op jit(solution)/shard_map/ppermute | solution.py:17
  143.7 8.0 %collective-permute-start.3 = (bf16[1,14,14,384]{3,2,1,0:T(8,128)(2,1)}, bf16[1,14,14,384]{3,2,1,0:T(8,128)(2,1)S(1)}, u32[]{:S(2)}, u32[]{:S(2)}) collective-permute-start(bf16[1,14,14,384]{3,2,1,0:T(8,128)(2,1)} %get-tuple-element.4679), channel_id=1, source_target_pairs={{0,32},{32,64},{64,96},{96,128},{128,160},{160,192},{192,224},{1,3... | collective-permute-start | bytes 451592 | tf_op jit(solution)/shard_map/ppermute | solution.py:17
  148.9 6.9 %collective-permute-start.17 = (bf16[1,14,14,384]{3,2,1,0:T(8,128)(2,1)}, bf16[1,14,14,384]{3,2,1,0:T(8,128)(2,1)S(1)}, u32[]{:S(2)}, u32[]{:S(2)}) collective-permute-start(bf16[1,14,14,384]{3,2,1,0:T(8,128)(2,1)} %get-tuple-element.4687), channel_id=1, source_target_pairs={{0,32},{32,64},{64,96},{96,128},{128,160},{160,192},{192,224},{1,3... | collective-permute-start | bytes 451592 | tf_op jit(solution)/shard_map/ppermute | solution.py:17
  152.4 7.0 %collective-permute-start.4 = (bf16[1,14,14,384]{3,2,1,0:T(8,128)(2,1)}, bf16[1,14,14,384]{3,2,1,0:T(8,128)(2,1)}, u32[]{:S(2)}, u32[]{:S(2)}) collective-permute-start(bf16[1,14,14,384]{3,2,1,0:T(8,128)(2,1)} %get-tuple-element.4680), channel_id=1, source_target_pairs={{0,32},{32,64},{64,96},{96,128},{128,160},{160,192},{192,224},{1,3... | collective-permute-start | bytes 451592 | tf_op jit(solution)/shard_map/ppermute | solution.py:17
  156.5 13.7 %collective-permute-start.18 = (bf16[1,14,14,384]{3,2,1,0:T(8,128)(2,1)}, bf16[1,14,14,384]{3,2,1,0:T(8,128)(2,1)S(1)}, u32[]{:S(2)}, u32[]{:S(2)}) collective-permute-start(bf16[1,14,14,384]{3,2,1,0:T(8,128)(2,1)} %get-tuple-element.4688), channel_id=1, source_target_pairs={{0,32},{32,64},{64,96},{96,128},{128,160},{160,192},{192,224},{1,3... | collective-permute-start | bytes 451592 | tf_op jit(solution)/shard_map/ppermute | solution.py:17
  161.0 12.2 %collective-permute-start.5 = (bf16[1,14,14,384]{3,2,1,0:T(8,128)(2,1)}, bf16[1,14,14,384]{3,2,1,0:T(8,128)(2,1)}, u32[]{:S(2)}, u32[]{:S(2)}) collective-permute-start(bf16[1,14,14,384]{3,2,1,0:T(8,128)(2,1)} %get-tuple-element.4681), channel_id=1, source_target_pairs={{0,32},{32,64},{64,96},{96,128},{128,160},{160,192},{192,224},{1,3... | collective-permute-start | bytes 451592 | tf_op jit(solution)/shard_map/ppermute | solution.py:17
  171.2 8.9 %collective-permute-start.19 = (bf16[1,14,14,384]{3,2,1,0:T(8,128)(2,1)}, bf16[1,14,14,384]{3,2,1,0:T(8,128)(2,1)}, u32[]{:S(2)}, u32[]{:S(2)}) collective-permute-start(bf16[1,14,14,384]{3,2,1,0:T(8,128)(2,1)} %get-tuple-element.4689), channel_id=1, source_target_pairs={{0,32},{32,64},{64,96},{96,128},{128,160},{160,192},{192,224},{1,3... | collective-permute-start | bytes 451592 | tf_op jit(solution)/shard_map/ppermute | solution.py:17
  174.9 12.7 %collective-permute-start.6 = (bf16[1,14,14,384]{3,2,1,0:T(8,128)(2,1)}, bf16[1,14,14,384]{3,2,1,0:T(8,128)(2,1)}, u32[]{:S(2)}, u32[]{:S(2)}) collective-permute-start(bf16[1,14,14,384]{3,2,1,0:T(8,128)(2,1)} %get-tuple-element.4682), channel_id=1, source_target_pairs={{0,32},{32,64},{64,96},{96,128},{128,160},{160,192},{192,224},{1,3... | collective-permute-start | bytes 451592 | tf_op jit(solution)/shard_map/ppermute | solution.py:17
  181.7 10.4 %collective-permute-start.20 = (bf16[1,14,14,384]{3,2,1,0:T(8,128)(2,1)}, bf16[1,14,14,384]{3,2,1,0:T(8,128)(2,1)}, u32[]{:S(2)}, u32[]{:S(2)}) collective-permute-start(bf16[1,14,14,384]{3,2,1,0:T(8,128)(2,1)} %get-tuple-element.4690), channel_id=1, source_target_pairs={{0,32},{32,64},{64,96},{96,128},{128,160},{160,192},{192,224},{1,3... | collective-permute-start | bytes 451592 | tf_op jit(solution)/shard_map/ppermute | solution.py:17
  193.1 7.8 %collective-permute-start.21 = (bf16[1,14,14,384]{3,2,1,0:T(8,128)(2,1)}, bf16[1,14,14,384]{3,2,1,0:T(8,128)(2,1)S(1)}, u32[]{:S(2)}, u32[]{:S(2)}) collective-permute-start(bf16[1,14,14,384]{3,2,1,0:T(8,128)(2,1)} %get-tuple-element.1815), channel_id=1, source_target_pairs={{32,0},{64,32},{96,64},{128,96},{160,128},{192,160},{224,192},{33,... | collective-permute-start | bytes 451592 | tf_op jit(solution)/shard_map/ppermute | solution.py:17
  201.6 7.9 %collective-permute-start.22 = (bf16[1,14,14,384]{3,2,1,0:T(8,128)(2,1)}, bf16[1,14,14,384]{3,2,1,0:T(8,128)(2,1)S(1)}, u32[]{:S(2)}, u32[]{:S(2)}) collective-permute-start(bf16[1,14,14,384]{3,2,1,0:T(8,128)(2,1)} %get-tuple-element.1818), channel_id=1, source_target_pairs={{32,0},{64,32},{96,64},{128,96},{160,128},{192,160},{224,192},{33,... | collective-permute-start | bytes 451592 | tf_op jit(solution)/shard_map/ppermute | solution.py:17
  210.3 8.2 %collective-permute-start.23 = (bf16[1,14,14,384]{3,2,1,0:T(8,128)(2,1)}, bf16[1,14,14,384]{3,2,1,0:T(8,128)(2,1)S(1)}, u32[]{:S(2)}, u32[]{:S(2)}) collective-permute-start(bf16[1,14,14,384]{3,2,1,0:T(8,128)(2,1)} %get-tuple-element.1821), channel_id=1, source_target_pairs={{32,0},{64,32},{96,64},{128,96},{160,128},{192,160},{224,192},{33,... | collective-permute-start | bytes 451592 | tf_op jit(solution)/shard_map/ppermute | solution.py:17
  219.1 7.9 %collective-permute-start.24 = (bf16[1,14,14,384]{3,2,1,0:T(8,128)(2,1)}, bf16[1,14,14,384]{3,2,1,0:T(8,128)(2,1)S(1)}, u32[]{:S(2)}, u32[]{:S(2)}) collective-permute-start(bf16[1,14,14,384]{3,2,1,0:T(8,128)(2,1)} %get-tuple-element.1824), channel_id=1, source_target_pairs={{32,0},{64,32},{96,64},{128,96},{160,128},{192,160},{224,192},{33,... | collective-permute-start | bytes 451592 | tf_op jit(solution)/shard_map/ppermute | solution.py:17
  225.1 31.2 %collective-permute-start.11 = (bf16[1,14,14,384]{3,2,1,0:T(8,128)(2,1)}, bf16[1,14,14,384]{3,2,1,0:T(8,128)(2,1)S(1)}, u32[]{:S(2)}, u32[]{:S(2)}) collective-permute-start(bf16[1,14,14,384]{3,2,1,0:T(8,128)(2,1)} %get-tuple-element.1805), channel_id=1, source_target_pairs={{32,0},{64,32},{96,64},{128,96},{160,128},{192,160},{224,192},{33,... | collective-permute-start | bytes 451592 | tf_op jit(solution)/shard_map/ppermute | solution.py:17
  227.7 41.5 %collective-permute-start.25 = (bf16[1,14,14,384]{3,2,1,0:T(8,128)(2,1)}, bf16[1,14,14,384]{3,2,1,0:T(8,128)(2,1)S(1)}, u32[]{:S(2)}, u32[]{:S(2)}) collective-permute-start(bf16[1,14,14,384]{3,2,1,0:T(8,128)(2,1)} %get-tuple-element.1827), channel_id=1, source_target_pairs={{32,0},{64,32},{96,64},{128,96},{160,128},{192,160},{224,192},{33,... | collective-permute-start | bytes 451592 | tf_op jit(solution)/shard_map/ppermute | solution.py:17
  267.3 13.7 %collective-permute-start.12 = (bf16[1,14,14,384]{3,2,1,0:T(8,128)(2,1)}, bf16[1,14,14,384]{3,2,1,0:T(8,128)(2,1)S(1)}, u32[]{:S(2)}, u32[]{:S(2)}) collective-permute-start(bf16[1,14,14,384]{3,2,1,0:T(8,128)(2,1)} %get-tuple-element.1808), channel_id=1, source_target_pairs={{32,0},{64,32},{96,64},{128,96},{160,128},{192,160},{224,192},{33,... | collective-permute-start | bytes 451592 | tf_op jit(solution)/shard_map/ppermute | solution.py:17
  279.1 8.2 %collective-permute-start.26 = (bf16[1,14,14,384]{3,2,1,0:T(8,128)(2,1)}, bf16[1,14,14,384]{3,2,1,0:T(8,128)(2,1)S(1)}, u32[]{:S(2)}, u32[]{:S(2)}) collective-permute-start(bf16[1,14,14,384]{3,2,1,0:T(8,128)(2,1)} %get-tuple-element.1830), channel_id=1, source_target_pairs={{32,0},{64,32},{96,64},{128,96},{160,128},{192,160},{224,192},{33,... | collective-permute-start | bytes 451592 | tf_op jit(solution)/shard_map/ppermute | solution.py:17
  282.1 22.5 %collective-permute-start.13 = (bf16[1,14,14,384]{3,2,1,0:T(8,128)(2,1)}, bf16[1,14,14,384]{3,2,1,0:T(8,128)(2,1)S(1)}, u32[]{:S(2)}, u32[]{:S(2)}) collective-permute-start(bf16[1,14,14,384]{3,2,1,0:T(8,128)(2,1)} %get-tuple-element.1813), channel_id=1, source_target_pairs={{32,0},{64,32},{96,64},{128,96},{160,128},{192,160},{224,192},{33,... | collective-permute-start | bytes 451592 | tf_op jit(solution)/shard_map/ppermute | solution.py:17
  288.0 16.7 %collective-permute-start.27 = (bf16[1,14,14,384]{3,2,1,0:T(8,128)(2,1)}, bf16[1,14,14,384]{3,2,1,0:T(8,128)(2,1)S(1)}, u32[]{:S(2)}, u32[]{:S(2)}) collective-permute-start(bf16[1,14,14,384]{3,2,1,0:T(8,128)(2,1)} %get-tuple-element.1835), channel_id=1, source_target_pairs={{32,0},{64,32},{96,64},{128,96},{160,128},{192,160},{224,192},{33,... | collective-permute-start | bytes 451592 | tf_op jit(solution)/shard_map/ppermute | solution.py:17
  (22 other events, 431.0 us)
Sparse Core Ops, SparseCore 0:
  18.3 79.5 all-gather.1
  313.1 146.5 all-reduce.108
where the time goes:
time: 478 us; the launch traced here: 470 us
  waiting for transfers between devices  256 us (54%)
  starting transfers between devices  82.8 us (17%)
  local copies, waits for them, and re-layouts  40.6 us (8%)
  loops' own time  30.9 us (6%)
  between operations  28.9 us (6%)
  other arithmetic  16.1 us (3%)
  matrix products  14.3 us (3%)
    unnamed x3, waiting for transfers between devices  143 us
    ppermute x28, starting transfers between devices, from_behind(): return lax.ppermute(x, axis, pairs)  82.7 us
    all_gather x1, waiting for transfers between devices, body(): gathered = lax.all_gather(weight_rows, 'dp', axis=2, tiled=True)  77.7 us
    ppermute x28, waiting for transfers between devices, from_behind(): return lax.ppermute(x, axis, pairs)  35.9 us
    cond x36, local copies, waits for them, and re-layouts  20.6 us
    another operation x16, loops' own time, body(): lax.cond(turn, backward_for(subnet, segment_inputs[subnet]), unchanged, s...  17.8 us
    another operation x14, loops' own time, body(): current = lax.cond(turn, forward_for(subnet), unchanged, current)  12.7 us
    dot_general x6, matrix products, block_forward(): jnp.dot(hidden.reshape(-1, width), weight, preferred_element_type=jnp.flo...  10.6 us
  transfers between devices with their start and end apart: 30, of which 13 were waited for; matrix products, arithmetic and copies ran while one was open for 12% of the time, Pallas kernels for 0%

commit v1 on v0

v1 whole, which is shorter than its diff:
```python
import functools

import jax
import jax.numpy as jnp
from jax import lax
from jax.experimental import pallas as pl
from jax.experimental.pallas import tpu as pltpu
from jax.sharding import PartitionSpec as P

first_decay = 0.9
second_decay = 0.999
learn_rate = 0.01
adam_epsilon = 1e-08
first_bias = 1.0 - 0.9**10
second_bias = 1.0 - 0.999**10

SIDE = 14
PITCH = 16
ROWS = SIDE * PITCH
LANES = 128
HEAD = 8 + 2 * PITCH
PADDED = 8 + (SIDE + 4) * PITCH + 8
BF = jnp.bfloat16
F32 = jnp.float32

ANY = pl.BlockSpec(memory_space=pl.ANY)
SMEM = pl.BlockSpec(memory_space=pltpu.SMEM)
PARAMS = pltpu.CompilerParams(vmem_limit_bytes=24 << 20)


def call(kernel, outs, in_specs, scratch, aliases=None, cost=2_000_000_000):
    return pl.pallas_call(
        kernel,
        out_shape=[jax.ShapeDtypeStruct(s, d) for s, d in outs],
        in_specs=in_specs,
        out_specs=[ANY] * len(outs),
        scratch_shapes=scratch,
        input_output_aliases=aliases or {},
        compiler_params=PARAMS,
        cost_estimate=pl.CostEstimate(flops=cost, bytes_accessed=1_000_000, transcendentals=0),
    )


def expand(slot, tall):
    shape = (768, 384) if tall else (384, 768)
    row = lax.broadcasted_iota(jnp.int32, shape, 1 if tall else 0)
    place = lax.broadcasted_iota(jnp.int32, shape, 0 if tall else 1)
    target = row + 12 * ((row * 10923) >> 17) + 12 * slot
    return jnp.where(place == target, 1.0, 0.0).astype(BF)


def keep_mask(shape):
    return (lax.broadcasted_iota(jnp.int32, shape, 0) & (PITCH - 1)) < SIDE


def conv_rows(pad, taps, group, flipped, emit):
    sign = -1 if flipped else 1
    cols = pl.ds(group * LANES, LANES)
    weights = [jnp.broadcast_to(taps[pl.ds(i, 1), cols], (PITCH, LANES)) for i in range(25)]
    for p in range(0, SIDE, 2):
        totals = [None, None]
        for da in range(-2, 4):
            for e in range(-2, 3):
                start = HEAD + PITCH * (p + da) + e
                window = pad[group, pl.ds(start, PITCH), :]
                for k in range(2):
                    a = da - k
                    if -2 <= a <= 2:
                        tap = (sign * a + 2) * 5 + (sign * e + 2)
                        term = weights[tap] * window
                        totals[k] = term if totals[k] is None else totals[k] + term
        emit(p, totals[0])
        emit(p + 1, totals[1])


def clear_pad(pad):
    for g in range(3):
        pad[g, pl.ds(0, HEAD), :] = jnp.zeros((HEAD, LANES), F32)
        pad[g, pl.ds(HEAD + ROWS, PADDED - HEAD - ROWS), :] = jnp.zeros(
            (PADDED - HEAD - ROWS, LANES), F32
        )


def fill_pad(pad, value):
    for g in range(3):
        pad[g, pl.ds(HEAD, ROWS), :] = value[:, g * LANES : (g + 1) * LANES]


def spread(image, flat):
    flat[...] = jnp.zeros(flat.shape, flat.dtype)
    for p in range(SIDE):
        flat[pl.ds(p * PITCH, SIDE), :] = image[p]


def live_of(meta, t):
    odd = (t & 1) == 1
    count = jnp.where(t < 2, meta[2], meta[3])
    return jnp.logical_or(jnp.logical_not(odd), count == 2)


def run_forward(meta, pad, flat, wsc, taps, hsc, dsc, after, skip_last):
    last = 1 + meta[3] if False else jnp.where(meta[3] == 2, 3, 2)
    fill_pad(pad, flat[...].astype(F32))

    def slot(t, carry):
        @pl.when(live_of(meta, t))
        def _():
            for g in range(3):

                def emit(p, u, g=g):
                    rows, cols = pl.ds(p * PITCH, PITCH), pl.ds(g * LANES, LANES)
                    s = 0.5 * jnp.tanh(0.5 * u) + 0.5
                    us = u * s
                    hsc[t, rows, cols] = us.astype(BF)
                    dsc[t, rows, cols] = s * (1.0 + (u - us))

                conv_rows(pad, taps.at[t], g, False, emit)
            after(t)

            def update():
                value = jnp.dot(hsc[t], wsc[t], preferred_element_type=F32)
                value = flat[...].astype(F32) + value
                rounded = jnp.where(keep_mask(value.shape), value, 0.0).astype(BF)
                flat[...] = rounded
                fill_pad(pad, rounded.astype(F32))

            if skip_last:
                pl.when(t != last)(update)
            else:
                update()

        return carry

    lax.fori_loop(0, 4, slot, 0)


def run_backward(meta, pad, flat, wsc, taps, dsc, ysc, before, after, skip_first):
    def slot(i, carry):
        t = 3 - i

        @pl.when(live_of(meta, t))
        def _():
            ysc[t] = flat[...]
            after(t)

            def chain():
                before(t)
                dh = lax.dot_general(
                    flat[...], wsc[t], (((1,), (1,)), ((), ())), preferred_element_type=F32
                )
                fill_pad(pad, dh * dsc[t])
                for g in range(3):

                    def emit(p, total, g=g):
                        rows, cols = pl.ds(p * PITCH, PITCH), pl.ds(g * LANES, LANES)
                        value = ysc[t, rows, cols].astype(F32) + total
                        keep = lax.broadcasted_iota(jnp.int32, value.shape, 0) < SIDE
                        flat[rows, cols] = jnp.where(keep, value, 0.0).astype(BF)

                    conv_rows(pad, taps.at[t], g, True, emit)

            if skip_first:
                pl.when(t != 0)(chain)
            else:
                chain()

        return carry

    lax.fori_loop(0, 4, slot, 0)


def each_live(meta, action):
    def slot(t, carry):
        pl.when(live_of(meta, t))(functools.partial(action, t))
        return carry

    lax.fori_loop(0, 4, slot, 0)


def first_kernel(meta, img, packed, kown, koth, y, wout, tout, hs, ds,
                 imsc, rsc, kbuf, wsc, taps, flat, pad, hsc, dsc, sems, hsems, dsems):
    core = meta[1]
    active = meta[0] == 0
    copies = [
        pltpu.make_async_copy(packed, rsc, sems.at[0]),
        pltpu.make_async_copy(kown, kbuf.at[0], sems.at[1]),
        pltpu.make_async_copy(koth, kbuf.at[1], sems.at[2]),
        pltpu.make_async_copy(img.at[0], imsc, sems.at[3]),
    ]
    for c in copies:
        c.start()
    clear_pad(pad)
    for c in copies[1:]:
        c.wait()
    for o in range(2):
        for j in range(2):
            taps[(2 * o + j + 2 * core) & 3] = kbuf[o, j].astype(F32)
    tcopy = pltpu.make_async_copy(taps, tout, sems.at[1])
    tcopy.start()
    copies[0].wait()
    for j in range(2):
        pick = expand(j, False)
        for o in range(2):
            rows = rsc[:, pl.ds(24 * o, 24), :].reshape(768, 384)
            wsc[(2 * o + j + 2 * core) & 3] = jnp.dot(
                pick, rows, preferred_element_type=F32
            ).astype(BF)
    wcopy = pltpu.make_async_copy(wsc, wout, sems.at[0])
    wcopy.start()

    def hcopy(t):
        return pltpu.make_async_copy(hsc.at[t], hs.at[t], hsems.at[t])

    def dcopy(t):
        return pltpu.make_async_copy(dsc.at[t], ds.at[t], dsems.at[t])

    @pl.when(active)
    def _():
        spread(imsc, flat)

        def after(t):
            hcopy(t).start()
            dcopy(t).start()

        run_forward(meta, pad, flat, wsc, taps, hsc, dsc, after, False)
        ycopy = pltpu.make_async_copy(flat, y, sems.at[3])
        ycopy.start()
        ycopy.wait()

        def finish(t):
            hcopy(t).wait()
            dcopy(t).wait()

        each_live(meta, finish)

    tcopy.wait()
    wcopy.wait()


def forward_kernel(step, meta, cur, win, tin, hin, din, y, hs, ds,
                   wsc, taps, flat, pad, hsc, dsc, sems, hsems, dsems):
    del hin, din

    def hcopy(t):
        return pltpu.make_async_copy(hsc.at[t], hs.at[t], hsems.at[t])

    def dcopy(t):
        return pltpu.make_async_copy(dsc.at[t], ds.at[t], dsems.at[t])

    @pl.when(meta[0] == step)
    def _():
        copies = [
            pltpu.make_async_copy(cur, flat, sems.at[0]),
            pltpu.make_async_copy(tin, taps, sems.at[1]),
            pltpu.make_async_copy(win, wsc, sems.at[2]),
        ]
        for c in copies:
            c.start()
        clear_pad(pad)
        for c in copies:
            c.wait()

        def after(t):
            hcopy(t).start()
            dcopy(t).start()

        run_forward(meta, pad, flat, wsc, taps, hsc, dsc, after, False)
        ycopy = pltpu.make_async_copy(flat, y, sems.at[0])
        ycopy.start()
        ycopy.wait()

        def finish(t):
            hcopy(t).wait()
            dcopy(t).wait()

        each_live(meta, finish)


def middle_kernel(step, meta, cur, cot, win, tin, hin, y, hs, ys,
                  imsc, wsc, taps, flat, pad, hsc, dsc, ysc, sems, hsems, ysems):
    del hin

    def hcopy(t):
        return pltpu.make_async_copy(hsc.at[t], hs.at[t], hsems.at[t])

    def yscopy(t):
        return pltpu.make_async_copy(ysc.at[t], ys.at[t], ysems.at[t])

    @pl.when(meta[0] == step)
    def _():
        copies = [
            pltpu.make_async_copy(cur, flat, sems.at[0]),
            pltpu.make_async_copy(tin, taps, sems.at[1]),
            pltpu.make_async_copy(win, wsc, sems.at[2]),
            pltpu.make_async_copy(cot.at[meta[1], 0], imsc, sems.at[3]),
        ]
        for c in copies:
            c.start()
        clear_pad(pad)
        for c in copies:
            c.wait()
        run_forward(
            meta, pad, flat, wsc, taps, hsc, dsc, lambda t: hcopy(t).start(), True
        )
        spread(imsc, flat)
        run_backward(
            meta, pad, flat, wsc, taps, dsc, ysc, lambda t: None, lambda t: yscopy(t).start(), False
        )
        ycopy = pltpu.make_async_copy(flat, y, sems.at[0])
        ycopy.start()
        ycopy.wait()

        def finish(t):
            hcopy(t).wait()
            yscopy(t).wait()

        each_live(meta, finish)


def backward_kernel(step, meta, cur, win, tin, ds, yin, y, ys,
                    wsc, taps, flat, pad, dsc, ysc, sems, dsems, ysems):
    del yin

    def dcopy(t):
        return pltpu.make_async_copy(ds.at[t], dsc.at[t], dsems.at[t])

    def yscopy(t):
        return pltpu.make_async_copy(ysc.at[t], ys.at[t], ysems.at[t])

    @pl.when(meta[0] == step)
    def _():
        copies = [
            pltpu.make_async_copy(cur, flat, sems.at[0]),
            pltpu.make_async_copy(win, wsc, sems.at[2]),
            pltpu.make_async_copy(tin, taps, sems.at[1]),
        ]
        for c in copies:
            c.start()
        each_live(meta, lambda t: dcopy(t).start())
        clear_pad(pad)
        for c in copies:
            c.wait()
        run_backward(
            meta, pad, flat, wsc, taps, dsc, ysc,
            lambda t: dcopy(t).wait(), lambda t: yscopy(t).start(), False,
        )
        ycopy = pltpu.make_async_copy(flat, y, sems.at[0])
        ycopy.start()
        ycopy.wait()
        each_live(meta, lambda t: yscopy(t).wait())


def last_kernel(meta, cur, win, tin, ds, hs, ys, send,
                wsc, taps, flat, pad, dsc, hsc, ysc, total, gsc, sems, dsems):
    core = meta[1]
    active = meta[0] == 0

    def dcopy(t):
        return pltpu.make_async_copy(ds.at[t], dsc.at[t], dsems.at[t])

    hcopy = pltpu.make_async_copy(hs, hsc, sems.at[3])
    hcopy.start()

    @pl.when(active)
    def _():
        copies = [
            pltpu.make_async_copy(cur, flat, sems.at[0]),
            pltpu.make_async_copy(win, wsc, sems.at[2]),
            pltpu.make_async_copy(tin, taps, sems.at[1]),
        ]
        for c in copies:
            c.start()
        each_live(meta, lambda t: dcopy(t).start())
        clear_pad(pad)
        for c in copies:
            c.wait()

        run_backward(
            meta, pad, flat, wsc, taps, dsc, ysc,
            lambda t: dcopy(t).wait(), lambda t: None, True,
        )
        dcopy(0).wait()

    @pl.when(jnp.logical_not(active))
    def _():
        copy = pltpu.make_async_copy(ys, ysc, sems.at[0])
        copy.start()
        copy.wait()

    hcopy.wait()

    def term(t, j):
        turned = lax.dot_general(
            expand(j, True), hsc[t], (((1,), (1,)), ((), ())), preferred_element_type=F32
        ).astype(BF)
        return jnp.dot(turned, ysc[t], preferred_element_type=F32)

    for o in range(2):
        base = (2 * o + 2 * core) & 3
        total[...] = term(base, 0)

        @pl.when(live_of(meta, base + 1))
        def _():
            total[...] += term(base + 1, 1)

        gsc[:, pl.ds(24 * o, 24), :] = total[...].astype(BF).reshape(32, 24, 384)
    out = pltpu.make_async_copy(gsc, send, sems.at[0])
    out.start()
    out.wait()


def prepare_kernel(meta, picks, weights, kernels, first, second, wown, woth, kown, koth,
                   wrows, frows, srows, sems):
    core = meta[1]
    copies = []

    def add(src, dst):
        copies.append(pltpu.make_async_copy(src, dst, sems.at[len(copies)]))

    for j in range(2):
        mine, theirs = picks[core, j], picks[1 - core, j]
        add(weights.at[j, mine], wown.at[j])
        add(weights.at[j, theirs], woth.at[j])
        add(kernels.at[j, mine], kown.at[j])
        add(kernels.at[j, theirs], koth.at[j])
        for n in range(2):
            add(weights.at[j, picks[n, j]], wrows.at[n, j])
            add(first.at[j, picks[n, j]], frows.at[n, j])
            add(second.at[j, picks[n, j]], srows.at[n, j])
    for c in copies:
        c.start()
    for c in copies:
        c.wait()


def sum_kernel(packed, own, other, rsc, osc, sem):
    copy = pltpu.make_async_copy(packed, rsc, sem.at[0])
    copy.start()
    copy.wait()
    total = rsc[0].astype(F32)
    for d in range(1, 32):
        total = total + rsc[d].astype(F32)
    osc[...] = total
    outs = [
        pltpu.make_async_copy(osc.at[pl.ds(0, 24)], own, sem.at[0]),
        pltpu.make_async_copy(osc.at[pl.ds(24, 24)], other, sem.at[1]),
    ]
    for c in outs:
        c.start()
    for c in outs:
        c.wait()


def adam_kernel(total_rows, meta, picks, own, other, wrows, frows, srows, new_w, new_f, new_s):
    core = meta[1]
    count = jnp.where(core == 0, meta[2], meta[3])
    for j in range(2):
        mine = own[pl.ds(12 * j, 12), :]
        theirs = other[pl.ds(12 * j, 12), :]
        same = picks[0, j] == picks[1, j]
        live = count > j
        for n in range(2):
            here = core == n
            grad = jnp.where(here, mine, theirs)
            rest = jnp.where(here, theirs, mine)
            grad = (grad + jnp.where(same, rest, jnp.zeros_like(rest))) / total_rows
            weight, one, two = wrows[n, j], frows[n, j], srows[n, j]
            next_one = first_decay * one + (1.0 - first_decay) * grad
            next_two = second_decay * two + (1.0 - second_decay) * grad * grad
            next_weight = (
                weight.astype(F32)
                - learn_rate
                * (next_one / first_bias)
                / (jnp.sqrt(next_two / second_bias) + adam_epsilon)
            ).astype(BF)
            new_w[n, j] = jnp.where(live, next_weight, weight)
            new_f[n, j] = jnp.where(live, next_one, one)
            new_s[n, j] = jnp.where(live, next_two, two)


def body(images, cotangent, picks, section_sizes, kernels, weights, first_moment, second_moment):
    width = images.shape[-1]
    own_segment = lax.axis_index("segment")
    segments = lax.axis_size("segment")
    parts = lax.axis_size("dp")
    total_rows = images.shape[0] * images.shape[1] * images.shape[2] * parts
    swap = [(s, s ^ 1) for s in range(segments)]
    ahead = [(s, (s + 2) % segments) for s in range(segments)]
    behind = [(s, (s - 2) % segments) for s in range(segments)]

    DMA = pltpu.SemaphoreType.DMA
    V = pltpu.VMEM
    state = (4, ROWS, width)
    flat_shape = (ROWS, width)
    s_w, s_t, s_flat = V((4, width, width), BF), V((4, 25, width), F32), V(flat_shape, BF)
    s_pad, s_h, s_d, s_y = V((3, PADDED, LANES), F32), V(state, BF), V(state, F32), V(state, BF)
    s_im, s_r = V((SIDE, SIDE, width), BF), V((32, 48, width), BF)

    core = own_segment & 1
    place = lax.broadcasted_iota(jnp.int32, (4,), 0)
    sizes_other = lax.ppermute(section_sizes, "segment", swap)
    early = jnp.where(place == 0, own_segment >> 1, core)

    rows_shape, kern_shape = (2, 12, width), (2, 25, width)
    four = (2, 2, 12, width)
    wown, woth, kown, koth_send, wrows, frows, srows = call(
        prepare_kernel,
        [(rows_shape, BF), (rows_shape, BF), (kern_shape, BF), (kern_shape, BF),
         (four, BF), (four, F32), (four, F32)],
        [SMEM, SMEM, ANY, ANY, ANY, ANY],
        [DMA((20,))],
        cost=1000,
    )(early, picks, weights, kernels, first_moment, second_moment)
    wrecv = lax.ppermute(woth, "segment", swap)
    koth = lax.ppermute(koth_send, "segment", swap)
    size_low = jnp.where(core == 0, section_sizes[0], sizes_other[0])
    size_high = jnp.where(core == 0, sizes_other[0], section_sizes[0])
    meta = jnp.where(place < 2, early, jnp.where(place == 2, size_low, size_high))

    message = jnp.concatenate([wown, wrecv], axis=0).reshape(1, 48, width)
    packed = lax.all_to_all(jnp.broadcast_to(message, (parts, 48, width)), "dp", 0, 0)

    y, wall, taps, hs, ds = call(
        first_kernel,
        [(flat_shape, BF), ((4, width, width), BF), ((4, 25, width), F32), (state, BF), (state, F32)],
        [SMEM, ANY, ANY, ANY, ANY],
        [s_im, s_r, V((2, 2, 25, width), BF), s_w, s_t, s_flat, s_pad, s_h, s_d,
         DMA((4,)), DMA((4,)), DMA((4,))],
    )(meta, images, packed, kown, koth)
    cur = lax.ppermute(y, "segment", ahead)
    for step in (1, 2):
        y, hs, ds = call(
            functools.partial(forward_kernel, step),
            [(flat_shape, BF), (state, BF), (state, F32)],
            [SMEM] + [ANY] * 5,
            [s_w, s_t, s_flat, s_pad, s_h, s_d, DMA((3,)), DMA((4,)), DMA((4,))],
            {4: 1, 5: 2},
        )(meta, cur, wall, taps, hs, ds)
        cur = lax.ppermute(y, "segment", ahead)
    y, hs, ys = call(
        functools.partial(middle_kernel, 3),
        [(flat_shape, BF), (state, BF), (state, BF)],
        [SMEM] + [ANY] * 5,
        [s_im, s_w, s_t, s_flat, s_pad, s_h, s_d, s_y, DMA((4,)), DMA((4,)), DMA((4,))],
        {5: 1},
    )(meta, cur, cotangent, wall, taps, hs)
    cur = lax.ppermute(y, "segment", behind)
    for step in (2, 1):
        y, ys = call(
            functools.partial(backward_kernel, step),
            [(flat_shape, BF), (state, BF)],
            [SMEM] + [ANY] * 5,
            [s_w, s_t, s_flat, s_pad, s_d, s_y, DMA((3,)), DMA((4,)), DMA((4,))],
            {5: 1},
        )(meta, cur, wall, taps, ds, ys)
        cur = lax.ppermute(y, "segment", behind)
    (send,) = call(
        last_kernel,
        [((32, 48, width), BF)],
        [SMEM] + [ANY] * 6,
        [s_w, s_t, s_flat, s_pad, s_d, s_h, s_y, V((768, width), F32), s_r, DMA((4,)), DMA((4,))],
    )(meta, cur, wall, taps, ds, hs, ys)
    landed = lax.all_to_all(send, "dp", 0, 0)
    own, for_other = call(
        sum_kernel,
        [((24, width), F32), ((24, width), F32)],
        [ANY],
        [s_r, V((48, width), F32), DMA((2,))],
    )(landed)
    other = lax.ppermute(for_other, "segment", swap)
    whole = pl.BlockSpec(memory_space=pltpu.VMEM)
    new_w, new_f, new_s = pl.pallas_call(
        functools.partial(adam_kernel, float(total_rows)),
        out_shape=[
            jax.ShapeDtypeStruct(four, BF),
            jax.ShapeDtypeStruct(four, F32),
            jax.ShapeDtypeStruct(four, F32),
        ],
        in_specs=[SMEM, SMEM] + [whole] * 5,
        out_specs=[whole] * 3,
        compiler_params=PARAMS,
    )(meta, picks, own, other, wrows, frows, srows)
    return (new_w, new_f, new_s)


def solution(mesh):
    return jax.shard_map(
        body,
        mesh=mesh,
        in_specs=(
            P("dp", None, None, None),
            P(None, "dp", None, None, None),
            P(None, "segment"),
            P("segment"),
            P("segment", None, None, None),
            P("segment", None, "dp", None),
            P("segment", None, "dp", None),
            P("segment", None, "dp", None),
        ),
        out_specs=(
            P(None, "segment", "dp", None),
            P(None, "segment", "dp", None),
            P(None, "segment", "dp", None),
        ),
        check_vma=False,
    )
```

time: 478 us -> 177 us (0.37)
  the two profiles are of different devices: /device:TPU:2 before, /device:TPU:1 now
where the time goes in v1:
time: 177 us
  waiting for transfers between devices  54.4 us (31%)
  starting transfers between devices  44.7 us (25%)
  blocking collectives  34.2 us (19%)
  Pallas kernels  23.8 us (13%)
  local copies, waits for them, and re-layouts  16.9 us (10%)
  between operations  2.63 us (1%)
    all_to_all x1, blocking collectives, body(): landed = lax.all_to_all(send, 'dp', 0, 0)  34.2 us
    all_to_all x1, waiting for transfers between devices, body(): lax.all_to_all(jnp.broadcast_to(message, (parts, 48, width)), 'dp', 0, 0)  28.5 us
    ppermute x3, starting transfers between devices, body(): cur = lax.ppermute(y, 'segment', behind)  20.3 us
    unnamed x41, local copies, waits for them, and re-layouts  13.7 us
    ppermute x3, waiting for transfers between devices, body(): cur = lax.ppermute(y, 'segment', ahead)  12.6 us
    ppermute x3, waiting for transfers between devices, body(): cur = lax.ppermute(y, 'segment', behind)  10.4 us
    all_to_all x1, starting transfers between devices, body(): lax.all_to_all(jnp.broadcast_to(message, (parts, 48, width)), 'dp', 0, 0)  9.63 us
    pallas_call x1, Pallas kernels, body(): call(last_kernel, [((32, 48, width), BF)], [SMEM] + [ANY] * 6, [s_w, s_t,...  9.05 us
  transfers between devices with their start and end apart: 11, of which 10 were waited for; matrix products, arithmetic and copies ran while one was open for 3% of the time, Pallas kernels for 0%

profile of v1, /device:TPU:1, one launch (start us, length us, event | category | flops | bytes accessed | tf_op | source)
XLA Modules:
  0.0 176.6 jit_solution(16219962286901984189)
XLA Ops:
  0.6 3.3 %collective-permute-start = (s32[1]{0:T(128)}, s32[1]{0:T(128)}, u32[]{:S(2)}, u32[]{:S(2)}) collective-permute-start(s32[1]{0:T(128)} %param.11), channel_id=1, source_target_pairs={{0,32},{32,0},{64,96},{96,64},{128,160},{160,128},{192,224},{224,1... | collective-permute-start | bytes 20 | tf_op jit(solution)/shard_map/ppermute | solution.py:501
  4.6 1.5 copy.26.weights
  7.8 2.0 %copy.28.first = f32[2,48,12,384]{3,2,1,0:T(8,128)} copy(f32[2,48,12,384]{3,1,2,0:T(8,128)S(1)} %copy-done.15) | data formatting | bytes 3538944 | tf_op args[6]
  9.8 2.0 %copy.29.second = f32[2,48,12,384]{3,2,1,0:T(8,128)} copy(f32[2,48,12,384]{3,1,2,0:T(8,128)S(1)} %copy-done.16) | data formatting | bytes 3538944 | tf_op args[7]
  13.0 1.7 copy-done
  14.7 1.7 copy-done.1
  16.3 1.3 shard_map.103
  23.2 9.6 %all-to-all-start = ((bf16[32,48,384]{2,1,0:T(8,128)(2,1)}), bf16[32,48,384]{2,1,0:T(8,128)(2,1)S(1)}, u32[]{:S(2)}, u32[]{:S(2)}) async-start(bf16[32,48,384]{2,1,0:T(8,128)(2,1)} %broadcast_in_dim.26), calls=%async_computation | async-start | bytes 2359296 | tf_op jit(solution)/shard_map/all_to_all | solution.py:521
  34.2 28.5 %all-to-all-done.packed = bf16[32,48,384]{2,1,0:T(8,128)(2,1)S(1)} async-done(((bf16[32,48,384]{2,1,0:T(8,128)(2,1)}), bf16[32,48,384]{2,1,0:T(8,128)(2,1)S(1)}, u32[]{:S(2)}, u32[]{:S(2)}) %all-to-all-start) | async-done | bytes 1179680 | tf_op jit(solution)/shard_map/all_to_all | solution.py:521
  62.7 8.8 %shard_map.104 = (bf16[224,384]{1,0:T(8,128)(2,1)S(1)}, bf16[4,384,384]{2,1,0:T(8,128)(2,1)S(1)}, f32[4,25,384]{2,1,0:T(8,128)S(1)}, bf16[4,224,384]{2,1,0:T(8,128)(2,1)S(1)}, f32[4,224,384]{2,1,0:T(8,128)S(1)}) custom-call(s32[4]{0:T(128)S(1)} %get-tuple-element.63.meta, bf16[1,14,14,384]{3,2,1,0:T(8,128)(2,1)S(1)} %copy-done.9, ...), custom_call_target="tpu_custom_call" | custom-call | flops 2000000000 | bytes 1000000 | tf_op jit(solution)/shard_map/pallas_call | solution.py:523
  71.6 5.5 %collective-permute-done.3.cur = bf16[224,384]{1,0:T(8,128)(2,1)S(1)} collective-permute-done((bf16[224,384]{1,0:T(8,128)(2,1)S(1)}, bf16[224,384]{1,0:T(8,128)(2,1)S(1)}, u32[]{:S(2)}, u32[]{:S(2)}) %collective-permute-start.3) | collective-permute-done | bytes 172064 | tf_op jit(solution)/shard_map/ppermute | solution.py:530
  77.7 2.5 %collective-permute-start.4 = (bf16[224,384]{1,0:T(8,128)(2,1)S(1)}, bf16[224,384]{1,0:T(8,128)(2,1)S(1)}, u32[]{:S(2)}, u32[]{:S(2)}) collective-permute-start(bf16[224,384]{1,0:T(8,128)(2,1)S(1)} %get-tuple-element.39), channel_id=1, source_target_pairs={{0,64},{32,96},{64,128},{96,160},{128,192},{160,224},{192,0},{224,... | collective-permute-start | bytes 516104 | tf_op jit(solution)/shard_map/ppermute | solution.py:539
  80.3 3.0 %collective-permute-done.4.cur = bf16[224,384]{1,0:T(8,128)(2,1)S(1)} collective-permute-done((bf16[224,384]{1,0:T(8,128)(2,1)S(1)}, bf16[224,384]{1,0:T(8,128)(2,1)S(1)}, u32[]{:S(2)}, u32[]{:S(2)}) %collective-permute-start.4) | collective-permute-done | bytes 172064 | tf_op jit(solution)/shard_map/ppermute | solution.py:539
  83.9 1.3 collective-permute-start.5
  85.3 4.2 %collective-permute-done.5.cur = bf16[224,384]{1,0:T(8,128)(2,1)S(1)} collective-permute-done((bf16[224,384]{1,0:T(8,128)(2,1)S(1)}, bf16[224,384]{1,0:T(8,128)(2,1)S(1)}, u32[]{:S(2)}, u32[]{:S(2)}) %collective-permute-start.5) | collective-permute-done | bytes 172064 | tf_op jit(solution)/shard_map/ppermute | solution.py:539
  90.3 13.9 %collective-permute-start.6 = (bf16[224,384]{1,0:T(8,128)(2,1)S(1)}, bf16[224,384]{1,0:T(8,128)(2,1)S(1)}, u32[]{:S(2)}, u32[]{:S(2)}) collective-permute-start(bf16[224,384]{1,0:T(8,128)(2,1)S(1)} %get-tuple-element.44), channel_id=1, source_target_pairs={{0,192},{32,224},{64,0},{96,32},{128,64},{160,96},{192,128},{224,1... | collective-permute-start | bytes 516104 | tf_op jit(solution)/shard_map/ppermute | solution.py:547
  104.2 2.4 %collective-permute-done.6.cur = bf16[224,384]{1,0:T(8,128)(2,1)S(1)} collective-permute-done((bf16[224,384]{1,0:T(8,128)(2,1)S(1)}, bf16[224,384]{1,0:T(8,128)(2,1)S(1)}, u32[]{:S(2)}, u32[]{:S(2)}) %collective-permute-start.6) | collective-permute-done | bytes 172064 | tf_op jit(solution)/shard_map/ppermute | solution.py:547
  107.2 3.2 %collective-permute-start.7 = (bf16[224,384]{1,0:T(8,128)(2,1)S(1)}, bf16[224,384]{1,0:T(8,128)(2,1)S(1)}, u32[]{:S(2)}, u32[]{:S(2)}) collective-permute-start(bf16[224,384]{1,0:T(8,128)(2,1)S(1)} %get-tuple-element.47), channel_id=1, source_target_pairs={{0,192},{32,224},{64,0},{96,32},{128,64},{160,96},{192,128},{224,1... | collective-permute-start | bytes 516104 | tf_op jit(solution)/shard_map/ppermute | solution.py:556
  110.4 3.0 %collective-permute-done.7.cur = bf16[224,384]{1,0:T(8,128)(2,1)S(1)} collective-permute-done((bf16[224,384]{1,0:T(8,128)(2,1)S(1)}, bf16[224,384]{1,0:T(8,128)(2,1)S(1)}, u32[]{:S(2)}, u32[]{:S(2)}) %collective-permute-start.7) | collective-permute-done | bytes 172064 | tf_op jit(solution)/shard_map/ppermute | solution.py:556
  114.0 3.2 %collective-permute-start.8 = (bf16[224,384]{1,0:T(8,128)(2,1)S(1)}, bf16[224,384]{1,0:T(8,128)(2,1)S(1)}, u32[]{:S(2)}, u32[]{:S(2)}) collective-permute-start(bf16[224,384]{1,0:T(8,128)(2,1)S(1)} %get-tuple-element.49), channel_id=1, source_target_pairs={{0,192},{32,224},{64,0},{96,32},{128,64},{160,96},{192,128},{224,1... | collective-permute-start | bytes 516104 | tf_op jit(solution)/shard_map/ppermute | solution.py:556
  117.2 5.1 %collective-permute-done.8.cur = bf16[224,384]{1,0:T(8,128)(2,1)S(1)} collective-permute-done((bf16[224,384]{1,0:T(8,128)(2,1)S(1)}, bf16[224,384]{1,0:T(8,128)(2,1)S(1)}, u32[]{:S(2)}, u32[]{:S(2)}) %collective-permute-start.8) | collective-permute-done | bytes 172064 | tf_op jit(solution)/shard_map/ppermute | solution.py:556
  122.3 9.0 %shard_map.110 = bf16[32,48,384]{2,1,0:T(8,128)(2,1)S(1)} custom-call(s32[4]{0:T(128)S(1)} %get-tuple-element.63.meta, bf16[224,384]{1,0:T(8,128)(2,1)S(1)} %collective-permute-done.8.cur, bf16[4,384,384]{2,1,0:T(8,128)(2,1)S(1)} %get-tuple-element.35.win, f32[4,25,384]{2,1,0:T(8,128)S(1)} %get-tuple-element.36.tin, ...), custom_call_target="tpu_custom_call" | custom-call | flops 2000000000 | bytes 1000000 | tf_op jit(solution)/shard_map/pallas_call | solution.py:557
  131.4 34.2 %all_to_all.10.packed = bf16[32,48,384]{2,1,0:T(8,128)(2,1)S(1)} all-to-all(bf16[32,48,384]{2,1,0:T(8,128)(2,1)S(1)} %shard_map.110), channel_id=1, replica_groups=mesh['segment'=8,'dp'=32] {'dp'}, dimensions={0} | all-to-all | bytes 2359296 | tf_op jit(solution)/shard_map/all_to_all | solution.py:563
  166.1 7.0 %collective-permute-start.9 = (f32[24,384]{1,0:T(8,128)S(1)}, f32[24,384]{1,0:T(8,128)S(1)}, u32[]{:S(2)}, u32[]{:S(2)}) collective-permute-start(f32[24,384]{1,0:T(8,128)S(1)} %get-tuple-element.53), channel_id=1, source_target_pairs={{0,32},{32,0},{64,96},{96,64},{128,160},{160,128},{192,224},{224,1... | collective-permute-start | bytes 110600 | tf_op jit(solution)/shard_map/ppermute | solution.py:570
  (57 shorter events, 16.2 us)
Async XLA Ops:
  0.6 11.2 %collective-permute-start = (s32[1]{0:T(128)}, s32[1]{0:T(128)}, u32[]{:S(2)}, u32[]{:S(2)}) collective-permute-start(s32[1]{0:T(128)} %param.11), channel_id=1, source_target_pairs={{0,32},{32,0},{64,96},{96,64},{128,160},{160,128},{192,224},{224,1... | collective-permute-start | bytes 20 | tf_op jit(solution)/shard_map/ppermute | solution.py:501
  4.6 1.8 %copy-start.14 = (bf16[2,48,25,384]{3,1,2,0:T(8,128)(2,1)S(1)}, bf16[2,48,25,384]{3,1,2,0:T(8,128)(2,1)}, u32[]{:S(2)}) copy-start(bf16[2,48,25,384]{3,1,2,0:T(8,128)(2,1)} %param.12) | copy-start | bytes 5529604
  6.3 1.5 copy-start.15
  7.8 2.0 %copy-start.16 = (f32[2,48,12,384]{3,1,2,0:T(8,128)S(1)}, f32[2,48,12,384]{3,1,2,0:T(8,128)}, u32[]{:S(2)}) copy-start(f32[2,48,12,384]{3,1,2,0:T(8,128)} %param.15) | copy-start | bytes 5308420
  9.8 3.2 %copy-start.8 = (s32[2,2]{1,0:T(2,128)S(1)}, s32[2,2]{1,0:T(2,128)}, u32[]{:S(2)}) copy-start(s32[2,2]{1,0:T(2,128)} %picks.3) | copy-start | bytes 52
  13.0 1.7 copy-start
  14.7 1.7 copy-start.1
  20.8 1.2 collective-permute-start.1
  23.2 9.6 %copy-start.13 = (bf16[2,25,384]{2,1,0:T(8,128)(2,1)S(1)}, bf16[2,25,384]{2,1,0:T(8,128)(2,1)}, u32[]{:S(2)}) copy-start(bf16[2,25,384]{2,1,0:T(8,128)(2,1)} %copy-done.12) | copy-start | bytes 115204
  23.2 39.5 %copy-start.9 = (bf16[1,14,14,384]{3,2,1,0:T(8,128)(2,1)S(1)}, bf16[1,14,14,384]{3,2,1,0:T(8,128)(2,1)}, u32[]{:S(2)}) copy-start(bf16[1,14,14,384]{3,2,1,0:T(8,128)(2,1)} %img.1) | copy-start | bytes 451588
  23.2 39.5 %copy-start.11 = (bf16[2,25,384]{2,1,0:T(8,128)(2,1)S(1)}, bf16[2,25,384]{2,1,0:T(8,128)(2,1)}, u32[]{:S(2)}) copy-start(bf16[2,25,384]{2,1,0:T(8,128)(2,1)} %copy-done.10) | copy-start | bytes 115204
  23.2 39.5 %all-to-all-start = ((bf16[32,48,384]{2,1,0:T(8,128)(2,1)}), bf16[32,48,384]{2,1,0:T(8,128)(2,1)S(1)}, u32[]{:S(2)}, u32[]{:S(2)}) async-start(bf16[32,48,384]{2,1,0:T(8,128)(2,1)} %broadcast_in_dim.26), calls=%async_computation | async-start | bytes 2359296 | tf_op jit(solution)/shard_map/all_to_all | solution.py:521
  32.8 1.4 collective-permute-start.2
  71.5 5.5 %collective-permute-start.3 = (bf16[224,384]{1,0:T(8,128)(2,1)S(1)}, bf16[224,384]{1,0:T(8,128)(2,1)S(1)}, u32[]{:S(2)}, u32[]{:S(2)}) collective-permute-start(bf16[224,384]{1,0:T(8,128)(2,1)S(1)} %get-tuple-element.34), channel_id=1, source_target_pairs={{0,64},{32,96},{64,128},{96,160},{128,192},{160,224},{192,0},{224,... | collective-permute-start | bytes 516104 | tf_op jit(solution)/shard_map/ppermute | solution.py:530
  77.7 5.5 %collective-permute-start.4 = (bf16[224,384]{1,0:T(8,128)(2,1)S(1)}, bf16[224,384]{1,0:T(8,128)(2,1)S(1)}, u32[]{:S(2)}, u32[]{:S(2)}) collective-permute-start(bf16[224,384]{1,0:T(8,128)(2,1)S(1)} %get-tuple-element.39), channel_id=1, source_target_pairs={{0,64},{32,96},{64,128},{96,160},{128,192},{160,224},{192,0},{224,... | collective-permute-start | bytes 516104 | tf_op jit(solution)/shard_map/ppermute | solution.py:539
  83.3 2.0 %copy-start.17 = (bf16[2,1,14,14,384]{4,0,3,2,1:T(2,128)(2,1)S(1)}, bf16[2,1,14,14,384]{4,0,3,2,1:T(2,128)(2,1)}, u32[]{:S(2)}) copy-start(bf16[2,1,14,14,384]{4,0,3,2,1:T(2,128)(2,1)} %param.9) | copy-start | bytes 903172
  83.9 5.5 %collective-permute-start.5 = (bf16[224,384]{1,0:T(8,128)(2,1)S(1)}, bf16[224,384]{1,0:T(8,128)(2,1)S(1)}, u32[]{:S(2)}, u32[]{:S(2)}) collective-permute-start(bf16[224,384]{1,0:T(8,128)(2,1)S(1)} %get-tuple-element.42), channel_id=1, source_target_pairs={{0,64},{32,96},{64,128},{96,160},{128,192},{160,224},{192,0},{224,... | collective-permute-start | bytes 516104 | tf_op jit(solution)/shard_map/ppermute | solution.py:539
  90.3 16.2 %collective-permute-start.6 = (bf16[224,384]{1,0:T(8,128)(2,1)S(1)}, bf16[224,384]{1,0:T(8,128)(2,1)S(1)}, u32[]{:S(2)}, u32[]{:S(2)}) collective-permute-start(bf16[224,384]{1,0:T(8,128)(2,1)S(1)} %get-tuple-element.44), channel_id=1, source_target_pairs={{0,192},{32,224},{64,0},{96,32},{128,64},{160,96},{192,128},{224,1... | collective-permute-start | bytes 516104 | tf_op jit(solution)/shard_map/ppermute | solution.py:547
  107.2 6.1 %collective-permute-start.7 = (bf16[224,384]{1,0:T(8,128)(2,1)S(1)}, bf16[224,384]{1,0:T(8,128)(2,1)S(1)}, u32[]{:S(2)}, u32[]{:S(2)}) collective-permute-start(bf16[224,384]{1,0:T(8,128)(2,1)S(1)} %get-tuple-element.47), channel_id=1, source_target_pairs={{0,192},{32,224},{64,0},{96,32},{128,64},{160,96},{192,128},{224,1... | collective-permute-start | bytes 516104 | tf_op jit(solution)/shard_map/ppermute | solution.py:556
  114.0 8.3 %collective-permute-start.8 = (bf16[224,384]{1,0:T(8,128)(2,1)S(1)}, bf16[224,384]{1,0:T(8,128)(2,1)S(1)}, u32[]{:S(2)}, u32[]{:S(2)}) collective-permute-start(bf16[224,384]{1,0:T(8,128)(2,1)S(1)} %get-tuple-element.49), channel_id=1, source_target_pairs={{0,192},{32,224},{64,0},{96,32},{128,64},{160,96},{192,128},{224,1... | collective-permute-start | bytes 516104 | tf_op jit(solution)/shard_map/ppermute | solution.py:556
  165.6 8.3 %copy-start.3 = (f32[2,2,12,384]{3,2,1,0:T(8,128)S(1)}, f32[2,2,12,384]{3,2,1,0:T(8,128)}, u32[]{:S(2)}) copy-start(f32[2,2,12,384]{3,2,1,0:T(8,128)} %copy-done.2) | copy-start | bytes 221188
  165.6 8.3 %copy-start.5 = (f32[2,2,12,384]{3,2,1,0:T(8,128)S(1)}, f32[2,2,12,384]{3,2,1,0:T(8,128)}, u32[]{:S(2)}) copy-start(f32[2,2,12,384]{3,2,1,0:T(8,128)} %copy-done.4) | copy-start | bytes 221188
  165.6 8.3 %copy-start.7 = (bf16[2,2,12,384]{3,2,1,0:T(8,128)(2,1)S(1)}, bf16[2,2,12,384]{3,2,1,0:T(8,128)(2,1)}, u32[]{:S(2)}) copy-start(bf16[2,2,12,384]{3,2,1,0:T(8,128)(2,1)} %copy-done.6) | copy-start | bytes 110596
  166.1 7.8 %collective-permute-start.9 = (f32[24,384]{1,0:T(8,128)S(1)}, f32[24,384]{1,0:T(8,128)S(1)}, u32[]{:S(2)}, u32[]{:S(2)}) collective-permute-start(f32[24,384]{1,0:T(8,128)S(1)} %get-tuple-element.53), channel_id=1, source_target_pairs={{0,32},{32,0},{64,96},{96,64},{128,160},{160,128},{192,224},{224,1... | collective-permute-start | bytes 110600 | tf_op jit(solution)/shard_map/ppermute | solution.py:570
  (5 other events, 3.1 us)

commit v2 on v1

v2 whole, which is shorter than its diff:
```python
import functools

import jax
import jax.numpy as jnp
from jax import lax
from jax.experimental import pallas as pl
from jax.experimental.pallas import tpu as pltpu
from jax.sharding import PartitionSpec as P

first_decay = 0.9
second_decay = 0.999
learn_rate = 0.01
adam_epsilon = 1e-08
first_bias = 1.0 - 0.9**10
second_bias = 1.0 - 0.999**10

SIDE = 14
PITCH = 16
ROWS = SIDE * PITCH
LANES = 128
HEAD = 8 + 2 * PITCH
PADDED = 8 + (SIDE + 4) * PITCH + 8
BF = jnp.bfloat16
F32 = jnp.float32

ANY = pl.BlockSpec(memory_space=pl.ANY)
SMEM = pl.BlockSpec(memory_space=pltpu.SMEM)
PARAMS = pltpu.CompilerParams(vmem_limit_bytes=24 << 20)


VMEM = pl.BlockSpec(memory_space=pltpu.VMEM)


def call(kernel, outs, in_specs, scratch, aliases=None, cost=2_000_000_000):
    return pl.pallas_call(
        kernel,
        out_shape=[jax.ShapeDtypeStruct(s, d) for s, d in outs],
        in_specs=in_specs,
        out_specs=[VMEM] * len(outs),
        scratch_shapes=scratch,
        input_output_aliases=aliases or {},
        compiler_params=PARAMS,
        cost_estimate=pl.CostEstimate(flops=cost, bytes_accessed=1_000_000, transcendentals=0),
    )


def keep_mask(shape):
    return (lax.broadcasted_iota(jnp.int32, shape, 0) & (PITCH - 1)) < SIDE


def conv_rows(pad, taps, group, flipped, emit):
    sign = -1 if flipped else 1
    cols = pl.ds(group * LANES, LANES)
    weights = [jnp.broadcast_to(taps[pl.ds(i, 1), cols], (PITCH, LANES)) for i in range(25)]
    for p in range(0, SIDE, 2):
        totals = [None, None]
        for da in range(-2, 4):
            for e in range(-2, 3):
                start = HEAD + PITCH * (p + da) + e
                window = pad[group, pl.ds(start, PITCH), :]
                for k in range(2):
                    a = da - k
                    if -2 <= a <= 2:
                        tap = (sign * a + 2) * 5 + (sign * e + 2)
                        term = weights[tap] * window
                        totals[k] = term if totals[k] is None else totals[k] + term
        emit(p, totals[0])
        emit(p + 1, totals[1])


def clear_pad(pad):
    for g in range(3):
        pad[g, pl.ds(0, HEAD), :] = jnp.zeros((HEAD, LANES), F32)
        pad[g, pl.ds(HEAD + ROWS, PADDED - HEAD - ROWS), :] = jnp.zeros(
            (PADDED - HEAD - ROWS, LANES), F32
        )


def fill_pad(pad, value):
    for g in range(3):
        pad[g, pl.ds(HEAD, ROWS), :] = value[:, g * LANES : (g + 1) * LANES]


def live_of(meta, t):
    odd = (t & 1) == 1
    count = jnp.where(t < 2, meta[2], meta[3])
    return jnp.logical_or(jnp.logical_not(odd), count == 2)


def run_forward(meta, pad, flat, wall, taps, hs, ds, skip_last):
    last = jnp.where(meta[3] == 2, 3, 2)
    fill_pad(pad, flat[...].astype(F32))

    def slot(t, carry):
        @pl.when(live_of(meta, t))
        def _():
            for g in range(3):

                def emit(p, u, g=g):
                    rows, cols = pl.ds(p * PITCH, PITCH), pl.ds(g * LANES, LANES)
                    s = 0.5 * jnp.tanh(0.5 * u) + 0.5
                    us = u * s
                    hs[t, rows, cols] = us.astype(BF)
                    ds[t, rows, cols] = s * (1.0 + (u - us))

                conv_rows(pad, taps.at[t], g, False, emit)

            def update():
                value = jnp.dot(hs[t], wall[t], preferred_element_type=F32)
                value = flat[...].astype(F32) + value
                rounded = jnp.where(keep_mask(value.shape), value, 0.0).astype(BF)
                flat[...] = rounded
                fill_pad(pad, rounded.astype(F32))

            if skip_last:
                pl.when(t != last)(update)
            else:
                update()

        return carry

    lax.fori_loop(0, 4, slot, 0)


def run_backward(meta, pad, flat, wall, taps, ds, ys, skip_first):
    def slot(i, carry):
        t = 3 - i

        @pl.when(live_of(meta, t))
        def _():
            ys[t] = flat[...]

            def chain():
                dh = lax.dot_general(
                    flat[...], wall[t], (((1,), (1,)), ((), ())), preferred_element_type=F32
                )
                fill_pad(pad, dh * ds[t])
                for g in range(3):

                    def emit(p, total, g=g):
                        rows, cols = pl.ds(p * PITCH, PITCH), pl.ds(g * LANES, LANES)
                        value = ys[t, rows, cols].astype(F32) + total
                        keep = lax.broadcasted_iota(jnp.int32, value.shape, 0) < SIDE
                        flat[rows, cols] = jnp.where(keep, value, 0.0).astype(BF)

                    conv_rows(pad, taps.at[t], g, True, emit)

            if skip_first:
                pl.when(t != 0)(chain)
            else:
                chain()

        return carry

    lax.fori_loop(0, 4, slot, 0)


def first_kernel(meta, img, packed, kown, koth, y, wall, taps, hs, ds, pad):
    core = meta[1]
    for o, kref in enumerate((kown, koth)):
        for j in range(2):
            taps[(2 * o + j + 2 * core) & 3] = kref[j].astype(F32)
    for o in range(2):
        base = (2 * o + 2 * core) & 3
        for i in range(16):
            one = packed[2 * i, pl.ds(24 * o, 24), :].astype(F32)
            two = packed[2 * i + 1, pl.ds(24 * o, 24), :].astype(F32)
            rows = pl.ds(24 * i, 24)
            wall[base, rows, :] = jnp.concatenate([one[:12], two[:12]], axis=0).astype(BF)
            wall[base + 1, rows, :] = jnp.concatenate([one[12:], two[12:]], axis=0).astype(BF)

    @pl.when(meta[0] == 0)
    def _():
        clear_pad(pad)
        y[...] = img[...]
        run_forward(meta, pad, y, wall, taps, hs, ds, False)


def forward_kernel(step, meta, cur, wall, taps, hin, din, y, hs, ds, pad):
    del hin, din

    @pl.when(meta[0] == step)
    def _():
        clear_pad(pad)
        y[...] = cur[...]
        run_forward(meta, pad, y, wall, taps, hs, ds, False)


def middle_kernel(step, meta, cur, cot, wall, taps, hin, din, y, hs, ys, ds, pad):
    del hin, din

    @pl.when(meta[0] == step)
    def _():
        clear_pad(pad)
        y[...] = cur[...]
        run_forward(meta, pad, y, wall, taps, hs, ds, True)
        y[...] = cot[...]
        run_backward(meta, pad, y, wall, taps, ds, ys, False)


def backward_kernel(step, meta, cur, wall, taps, ds, yin, y, ys, pad):
    del yin

    @pl.when(meta[0] == step)
    def _():
        clear_pad(pad)
        y[...] = cur[...]
        run_backward(meta, pad, y, wall, taps, ds, ys, False)


def last_kernel(meta, cur, wall, taps, ds, hs, yin, send, ys, flat, pad, total):
    del yin
    core = meta[1]

    @pl.when(meta[0] == 0)
    def _():
        clear_pad(pad)
        flat[...] = cur[...]
        run_backward(meta, pad, flat, wall, taps, ds, ys, True)

    def term(t):
        return lax.dot_general(
            hs[t], ys[t], (((0,), (0,)), ((), ())), preferred_element_type=F32
        )

    for o in range(2):
        base = (2 * o + 2 * core) & 3
        live = live_of(meta, base + 1)
        total[0] = term(base)

        @pl.when(live)
        def _():
            total[1] = term(base + 1)

        @pl.when(jnp.logical_not(live))
        def _():
            total[1] = jnp.zeros(total.shape[1:], F32)

        for i in range(16):
            rows = pl.ds(24 * i, 24)
            one, two = total[0, rows, :], total[1, rows, :]
            place = pl.ds(24 * o, 24)
            send[2 * i, place, :] = jnp.concatenate([one[:12], two[:12]], axis=0).astype(BF)
            send[2 * i + 1, place, :] = jnp.concatenate([one[12:], two[12:]], axis=0).astype(BF)


def weight_kernel(meta, picks, weights, own, oth, buf, wide, rows, sems):
    core = meta[1]
    copies = []
    for k, out in enumerate((own, oth)):
        for j in range(2):
            op = picks[core if k == 0 else 1 - core, j]
            group = pl.ds(pl.multiple_of((op >> 3) << 3, 8), 8)
            copies.append(
                pltpu.make_async_copy(
                    weights.at[j, :, group, :], buf.at[2 * k + j], sems.at[2 * k + j]
                )
            )
            copies[-1].start()
    for k, out in enumerate((own, oth)):
        for j in range(2):
            op = picks[core if k == 0 else 1 - core, j]
            copies[2 * k + j].wait()
            wide[...] = buf[2 * k + j].astype(F32)
            for r in range(12):
                rows[k, pl.ds(12 * j + r, 1), :] = wide[r, pl.ds(op & 7, 1), :]
        out[...] = rows[k].astype(BF)


def table_kernel(meta, picks, kernels, first, second, kown, koth, fown, foth, sown, soth,
                 kbuf, kwide, krows, mbuf, sems):
    core = meta[1]
    picked = []
    for k, (kout, fout, sout) in enumerate(((kown, fown, sown), (koth, foth, soth))):
        for j in range(2):
            op = picks[core if k == 0 else 1 - core, j]
            group = pl.ds(pl.multiple_of((op >> 3) << 3, 8), 8)
            i = 2 * k + j
            copies = [
                pltpu.make_async_copy(kernels.at[j, :, group, :], kbuf.at[i], sems.at[i]),
                pltpu.make_async_copy(first.at[j, :, group, :], mbuf.at[i], sems.at[4 + i]),
                pltpu.make_async_copy(second.at[j, :, group, :], mbuf.at[4 + i], sems.at[8 + i]),
            ]
            picked.append((copies, op & 7, kout, fout, sout, i, j))
            for c in copies:
                c.start()
    for copies, lane, kout, fout, sout, i, j in picked:
        copies[0].wait()
        kwide[...] = kbuf[i].astype(F32)
        for r in range(25):
            krows[pl.ds(r, 1), :] = kwide[r, pl.ds(lane, 1), :]
        kout[j] = krows[...].astype(BF)
        copies[1].wait()
        copies[2].wait()
        for r in range(12):
            fout[pl.ds(2 * r + j, 1), :] = mbuf[i, r, pl.ds(lane, 1), :]
            sout[pl.ds(2 * r + j, 1), :] = mbuf[4 + i, r, pl.ds(lane, 1), :]


def message_kernel(own, recv, out):
    for o, ref in enumerate((own, recv)):
        value = ref[...]
        for d in range(32):
            out[d, pl.ds(24 * o, 24), :] = value


def sum_kernel(packed, own, other, wide):
    total = packed[0].astype(F32)
    for d in range(1, 32):
        total = total + packed[d].astype(F32)
    wide[...] = total
    for o, out in enumerate((own, other)):
        for j in range(2):
            for r in range(12):
                out[pl.ds(2 * r + j, 1), :] = wide[pl.ds(24 * o + 12 * j + r, 1), :]


def adam_kernel(total_rows, meta, picks, mine, theirs, wown, woth, fown, foth, sown, soth,
                new_w, new_f, new_s, wide):
    core = meta[1]
    count = jnp.where(core == 0, meta[2], meta[3])
    odd = (lax.broadcasted_iota(jnp.int32, mine.shape, 0) & 1) == 1
    same_first = jnp.where(picks[0, 0] == picks[1, 0], 1.0, 0.0)
    same_second = jnp.where(picks[0, 1] == picks[1, 1], 1.0, 0.0)
    same = jnp.where(odd, same_second, same_first) > 0.5
    live = jnp.where(odd, count, 2) == 2
    for k, (wref, fref, sref) in enumerate(((wown, fown, sown), (woth, foth, soth))):
        n = core if k == 0 else 1 - core
        grad, rest = (mine[...], theirs[...]) if k == 0 else (theirs[...], mine[...])
        grad = (grad + jnp.where(same, rest, jnp.zeros_like(rest))) / total_rows
        source = wref[...].astype(F32)
        for j in range(2):
            for r in range(12):
                wide[pl.ds(2 * r + j, 1), :] = source[12 * j + r : 12 * j + r + 1, :]
        weight, one, two = wide[...], fref[...], sref[...]
        next_one = first_decay * one + (1.0 - first_decay) * grad
        next_two = second_decay * two + (1.0 - second_decay) * grad * grad
        next_weight = weight - learn_rate * (next_one / first_bias) / (
            jnp.sqrt(next_two / second_bias) + adam_epsilon
        )
        out_w = jnp.where(live, next_weight, weight)
        out_f = jnp.where(live, next_one, one)
        out_s = jnp.where(live, next_two, two)
        for r in range(12):
            new_w[n, r] = out_w[2 * r : 2 * r + 2].astype(BF)
            new_f[n, r] = out_f[2 * r : 2 * r + 2]
            new_s[n, r] = out_s[2 * r : 2 * r + 2]


def body(images, cotangent, picks, section_sizes, kernels, weights, first_moment, second_moment):
    width = images.shape[-1]
    own_segment = lax.axis_index("segment")
    segments = lax.axis_size("segment")
    parts = lax.axis_size("dp")
    total_rows = images.shape[0] * images.shape[1] * images.shape[2] * parts
    swap = [(s, s ^ 1) for s in range(segments)]
    ahead = [(s, (s + 2) % segments) for s in range(segments)]
    behind = [(s, (s - 2) % segments) for s in range(segments)]

    DMA = pltpu.SemaphoreType.DMA
    V = pltpu.VMEM
    state = (4, ROWS, width)
    flat_shape = (ROWS, width)
    s_pad = V((3, PADDED, LANES), F32)
    pair, square, tap_shape = (24, width), (4, width, width), (4, 25, width)

    core = own_segment & 1
    place = lax.broadcasted_iota(jnp.int32, (4,), 0)
    early = jnp.where(place == 0, own_segment >> 1, core)
    sizes_other = lax.ppermute(section_sizes, "segment", swap)

    wown, woth = call(
        weight_kernel,
        [(pair, BF), (pair, BF)],
        [SMEM, SMEM, ANY],
        [V((4, 12, 8, width), BF), V((12, 8, width), F32), V((2, 24, width), F32), DMA((4,))],
        cost=1000,
    )(early, picks, weights.transpose(0, 2, 1, 3))
    wrecv = lax.ppermute(woth, "segment", swap)
    (message,) = call(message_kernel, [((32, 48, width), BF)], [VMEM, VMEM], [], cost=1000)(
        wown, wrecv
    )
    packed = lax.all_to_all(message, "dp", 0, 0)
    kown, kother, fown, foth, sown, soth = call(
        table_kernel,
        [((2, 25, width), BF)] * 2 + [(pair, F32)] * 4,
        [SMEM, SMEM, ANY, ANY, ANY],
        [V((4, 25, 8, width), BF), V((25, 8, width), F32), V((25, width), F32),
         V((8, 12, 8, width), F32), DMA((12,))],
    )(
        early,
        picks,
        kernels.transpose(0, 2, 1, 3),
        first_moment.transpose(0, 2, 1, 3),
        second_moment.transpose(0, 2, 1, 3),
    )
    koth = lax.ppermute(kother, "segment", swap)
    size_low = jnp.where(core == 0, section_sizes[0], sizes_other[0])
    size_high = jnp.where(core == 0, sizes_other[0], section_sizes[0])
    meta = jnp.where(place < 2, early, jnp.where(place == 2, size_low, size_high))
    edges = ((0, 0), (0, PITCH - SIDE), (0, 0))
    img = jnp.pad(images[0], edges).reshape(flat_shape)
    chosen = lax.dynamic_index_in_dim(cotangent[:, 0], core, 0, keepdims=False)
    cot = jnp.pad(chosen, edges).reshape(flat_shape)

    y, wall, taps, hs, ds = call(
        first_kernel,
        [(flat_shape, BF), (square, BF), (tap_shape, F32), (state, BF), (state, F32)],
        [SMEM] + [VMEM] * 4,
        [s_pad],
    )(meta, img, packed, kown, koth)
    cur = lax.ppermute(y, "segment", ahead)
    for step in (1, 2):
        y, hs, ds = call(
            functools.partial(forward_kernel, step),
            [(flat_shape, BF), (state, BF), (state, F32)],
            [SMEM] + [VMEM] * 5,
            [s_pad],
            {4: 1, 5: 2},
        )(meta, cur, wall, taps, hs, ds)
        cur = lax.ppermute(y, "segment", ahead)
    y, hs, ys, ds = call(
        functools.partial(middle_kernel, 3),
        [(flat_shape, BF), (state, BF), (state, BF), (state, F32)],
        [SMEM] + [VMEM] * 6,
        [s_pad],
        {5: 1, 6: 3},
    )(meta, cur, cot, wall, taps, hs, ds)
    cur = lax.ppermute(y, "segment", behind)
    for step in (2, 1):
        y, ys = call(
            functools.partial(backward_kernel, step),
            [(flat_shape, BF), (state, BF)],
            [SMEM] + [VMEM] * 5,
            [s_pad],
            {5: 1},
        )(meta, cur, wall, taps, ds, ys)
        cur = lax.ppermute(y, "segment", behind)
    send, _ = call(
        last_kernel,
        [((32, 48, width), BF), (state, BF)],
        [SMEM] + [VMEM] * 6,
        [V(flat_shape, BF), s_pad, V((2, width, width), F32)],
        {6: 1},
    )(meta, cur, wall, taps, ds, hs, ys)
    landed = lax.all_to_all(send, "dp", 0, 0)
    own, for_other = call(
        sum_kernel, [(pair, F32), (pair, F32)], [VMEM], [V((48, width), F32)]
    )(landed)
    other = lax.ppermute(for_other, "segment", swap)
    rows = (2, 12, 2, width)
    news = call(
        functools.partial(adam_kernel, float(total_rows)),
        [(rows, BF), (rows, F32), (rows, F32)],
        [SMEM, SMEM] + [VMEM] * 8,
        [V(pair, F32)],
    )(meta, picks, own, other, wown, woth, fown, foth, sown, soth)
    return tuple(new.transpose(0, 2, 1, 3) for new in news)


def solution(mesh):
    return jax.shard_map(
        body,
        mesh=mesh,
        in_specs=(
            P("dp", None, None, None),
            P(None, "dp", None, None, None),
            P(None, "segment"),
            P("segment"),
            P("segment", None, None, None),
            P("segment", None, "dp", None),
            P("segment", None, "dp", None),
            P("segment", None, "dp", None),
        ),
        out_specs=(
            P(None, "segment", "dp", None),
            P(None, "segment", "dp", None),
            P(None, "segment", "dp", None),
        ),
        check_vma=False,
    )
```

time: 177 us -> 147 us (0.83)
  Pallas kernels: 23.8 us -> 14.9 us
  local copies, waits for them, and re-layouts: 16.9 us -> 9.19 us
  starting transfers between devices: 44.7 us -> 37.8 us
  waiting for transfers between devices: 54.4 us -> 48.7 us
    pallas_call x5 -> x7, Pallas kernels: 20.4 us -> 12 us  [the longest x1 3.69 us: body(): call(last_kernel, [((32, 48, width), BF), (state, BF)], [SMEM] + [VMEM] *...]
    ppermute x3, starting transfers between devices: 20.3 us -> 13.6 us  [body(): cur = lax.ppermute(y, 'segment', behind)]
    all_to_all x1, waiting for transfers between devices: 28.5 us -> 22.7 us  [body(): packed = lax.all_to_all(message, 'dp', 0, 0)]
    unnamed x41 -> x49, local copies, waits for them, and re-layouts: 13.7 us -> 8.83 us
    pallas_call x3 -> x0, local copies, waits for them, and re-layouts: 1.99 us -> none  [body(): pl.pallas_call(functools.partial(adam_kernel, float(total_rows)), out_sha...]
  transfers between devices with their start and end apart: 11 -> 11, of which waited for: 10 -> 11; matrix products, arithmetic and copies ran while one was open for 3% -> 0% of each run, Pallas kernels for 0% -> 1%
where the time goes in v2:
time: 147 us
  waiting for transfers between devices  48.7 us (33%)
  starting transfers between devices  37.8 us (26%)
  blocking collectives  33.3 us (23%)
  Pallas kernels  14.9 us (10%)
  local copies, waits for them, and re-layouts  9.19 us (6%)
  between operations  2.81 us (2%)
    all_to_all x1, blocking collectives, body(): landed = lax.all_to_all(send, 'dp', 0, 0)  33.3 us
    all_to_all x1, waiting for transfers between devices, body(): packed = lax.all_to_all(message, 'dp', 0, 0)  22.7 us
    ppermute x3, waiting for transfers between devices, body(): cur = lax.ppermute(y, 'segment', ahead)  13.8 us
    ppermute x3, starting transfers between devices, body(): cur = lax.ppermute(y, 'segment', behind)  13.6 us
    all_to_all x1, starting transfers between devices, body(): packed = lax.all_to_all(message, 'dp', 0, 0)  9.63 us
    ppermute x3, waiting for transfers between devices, body(): cur = lax.ppermute(y, 'segment', behind)  9.41 us
    unnamed x49, local copies, waits for them, and re-layouts  8.83 us
    ppermute x1, starting transfers between devices, body(): other = lax.ppermute(for_other, 'segment', swap)  7.9 us
  transfers between devices with their start and end apart: 11, of which 11 were waited for; matrix products, arithmetic and copies ran while one was open for 0% of the time, Pallas kernels for 1%

profile of v2, /device:TPU:1, one launch (start us, length us, event | category | flops | bytes accessed | tf_op | source)
XLA Modules:
  0.0 146.8 jit_solution(10216902799112307555)
XLA Ops:
  0.6 3.3 %collective-permute-start = (s32[1]{0:T(128)}, s32[1]{0:T(128)}, u32[]{:S(2)}, u32[]{:S(2)}) collective-permute-start(s32[1]{0:T(128)} %param.11), channel_id=1, source_target_pairs={{0,32},{32,0},{64,96},{96,64},{128,160},{160,128},{192,224},{224,1... | collective-permute-start | bytes 20 | tf_op jit(solution)/shard_map/ppermute | solution.py:370
  6.2 1.2 copy-done.1
  10.0 1.1 shard_map.104
  11.2 9.6 %all-to-all-start = ((bf16[32,48,384]{2,1,0:T(8,128)(2,1)}), bf16[32,48,384]{2,1,0:T(8,128)(2,1)S(1)}, u32[]{:S(2)}, u32[]{:S(2)}) async-start(bf16[32,48,384]{2,1,0:T(8,128)(2,1)} %shard_map.104), calls=%async_computation | async-start | bytes 2359296 | tf_op jit(solution)/shard_map/all_to_all | solution.py:383
  20.9 1.5 copy-done.5
  22.3 1.5 %copy-done.6 = f32[2,48,12,384]{3,1,2,0:T(8,128)S(1)} copy-done((f32[2,48,12,384]{3,1,2,0:T(8,128)S(1)}, f32[2,48,12,384]{3,1,2,0:T(8,128)}, u32[]{:S(2)}) %copy-start.6) | copy-done | bytes 1769496
  23.8 1.2 shard_map.105
  27.7 22.7 %all-to-all-done.packed = bf16[32,48,384]{2,1,0:T(8,128)(2,1)S(1)} async-done(((bf16[32,48,384]{2,1,0:T(8,128)(2,1)}), bf16[32,48,384]{2,1,0:T(8,128)(2,1)S(1)}, u32[]{:S(2)}, u32[]{:S(2)}) %all-to-all-start) | async-done | bytes 1179680 | tf_op jit(solution)/shard_map/all_to_all | solution.py:383
  51.2 3.7 %shard_map.106 = (bf16[224,384]{1,0:T(8,128)(2,1)S(1)}, bf16[4,384,384]{2,1,0:T(8,128)(2,1)S(1)}, f32[4,25,384]{2,1,0:T(8,128)S(1)}, bf16[4,224,384]{2,1,0:T(8,128)(2,1)S(1)}, f32[4,224,384]{2,1,0:T(8,128)S(1)}) custom-call(s32[4]{0:T(128)S(1)} %get-tuple-element.69.meta, bf16[224,384]{1,0:T(8,128)(2,1)S(1)} %bitcast.18, ...), custom_call_target="tpu_custom_call" | custom-call | flops 2000000000 | bytes 1000000 | tf_op jit(solution)/shard_map/pallas_call | solution.py:406
  55.0 5.5 %collective-permute-done.3.cur = bf16[224,384]{1,0:T(8,128)(2,1)S(1)} collective-permute-done((bf16[224,384]{1,0:T(8,128)(2,1)S(1)}, bf16[224,384]{1,0:T(8,128)(2,1)S(1)}, u32[]{:S(2)}, u32[]{:S(2)}) %collective-permute-start.3) | collective-permute-done | bytes 172064 | tf_op jit(solution)/shard_map/ppermute | solution.py:412
  61.0 1.8 %collective-permute-start.4 = (bf16[224,384]{1,0:T(8,128)(2,1)S(1)}, bf16[224,384]{1,0:T(8,128)(2,1)S(1)}, u32[]{:S(2)}, u32[]{:S(2)}) collective-permute-start(bf16[224,384]{1,0:T(8,128)(2,1)S(1)} %get-tuple-element.45), channel_id=1, source_target_pairs={{0,64},{32,96},{64,128},{96,160},{128,192},{160,224},{192,0},{224,... | collective-permute-start | bytes 516104 | tf_op jit(solution)/shard_map/ppermute | solution.py:421
  62.8 3.7 %collective-permute-done.4.cur = bf16[224,384]{1,0:T(8,128)(2,1)S(1)} collective-permute-done((bf16[224,384]{1,0:T(8,128)(2,1)S(1)}, bf16[224,384]{1,0:T(8,128)(2,1)S(1)}, u32[]{:S(2)}, u32[]{:S(2)}) %collective-permute-start.4) | collective-permute-done | bytes 172064 | tf_op jit(solution)/shard_map/ppermute | solution.py:421
  68.9 4.6 %collective-permute-done.5.cur = bf16[224,384]{1,0:T(8,128)(2,1)S(1)} collective-permute-done((bf16[224,384]{1,0:T(8,128)(2,1)S(1)}, bf16[224,384]{1,0:T(8,128)(2,1)S(1)}, u32[]{:S(2)}, u32[]{:S(2)}) %collective-permute-start.5) | collective-permute-done | bytes 172064 | tf_op jit(solution)/shard_map/ppermute | solution.py:421
  73.4 1.1 copy-done.10
  75.1 7.2 %collective-permute-start.6 = (bf16[224,384]{1,0:T(8,128)(2,1)S(1)}, bf16[224,384]{1,0:T(8,128)(2,1)S(1)}, u32[]{:S(2)}, u32[]{:S(2)}) collective-permute-start(bf16[224,384]{1,0:T(8,128)(2,1)S(1)} %get-tuple-element.51), channel_id=1, source_target_pairs={{0,192},{32,224},{64,0},{96,32},{128,64},{160,96},{192,128},{224,1... | collective-permute-start | bytes 516104 | tf_op jit(solution)/shard_map/ppermute | solution.py:429
  82.3 2.4 %collective-permute-done.6.cur = bf16[224,384]{1,0:T(8,128)(2,1)S(1)} collective-permute-done((bf16[224,384]{1,0:T(8,128)(2,1)S(1)}, bf16[224,384]{1,0:T(8,128)(2,1)S(1)}, u32[]{:S(2)}, u32[]{:S(2)}) %collective-permute-start.6) | collective-permute-done | bytes 172064 | tf_op jit(solution)/shard_map/ppermute | solution.py:429
  85.4 3.2 %collective-permute-start.7 = (bf16[224,384]{1,0:T(8,128)(2,1)S(1)}, bf16[224,384]{1,0:T(8,128)(2,1)S(1)}, u32[]{:S(2)}, u32[]{:S(2)}) collective-permute-start(bf16[224,384]{1,0:T(8,128)(2,1)S(1)} %get-tuple-element.54), channel_id=1, source_target_pairs={{0,192},{32,224},{64,0},{96,32},{128,64},{160,96},{192,128},{224,1... | collective-permute-start | bytes 516104 | tf_op jit(solution)/shard_map/ppermute | solution.py:438
  88.6 3.1 %collective-permute-done.7.cur = bf16[224,384]{1,0:T(8,128)(2,1)S(1)} collective-permute-done((bf16[224,384]{1,0:T(8,128)(2,1)S(1)}, bf16[224,384]{1,0:T(8,128)(2,1)S(1)}, u32[]{:S(2)}, u32[]{:S(2)}) %collective-permute-start.7) | collective-permute-done | bytes 172064 | tf_op jit(solution)/shard_map/ppermute | solution.py:438
  92.3 3.2 %collective-permute-start.8 = (bf16[224,384]{1,0:T(8,128)(2,1)S(1)}, bf16[224,384]{1,0:T(8,128)(2,1)S(1)}, u32[]{:S(2)}, u32[]{:S(2)}) collective-permute-start(bf16[224,384]{1,0:T(8,128)(2,1)S(1)} %get-tuple-element.56), channel_id=1, source_target_pairs={{0,192},{32,224},{64,0},{96,32},{128,64},{160,96},{192,128},{224,1... | collective-permute-start | bytes 516104 | tf_op jit(solution)/shard_map/ppermute | solution.py:438
  95.5 3.9 %collective-permute-done.8.cur = bf16[224,384]{1,0:T(8,128)(2,1)S(1)} collective-permute-done((bf16[224,384]{1,0:T(8,128)(2,1)S(1)}, bf16[224,384]{1,0:T(8,128)(2,1)S(1)}, u32[]{:S(2)}, u32[]{:S(2)}) %collective-permute-start.8) | collective-permute-done | bytes 172064 | tf_op jit(solution)/shard_map/ppermute | solution.py:438
  99.4 3.7 %shard_map.112 = (bf16[32,48,384]{2,1,0:T(8,128)(2,1)S(1)}, bf16[4,224,384]{2,1,0:T(8,128)(2,1)S(1)}) custom-call(s32[4]{0:T(128)S(1)} %get-tuple-element.69.meta, bf16[224,384]{1,0:T(8,128)(2,1)S(1)} %collective-permute-done.8.cur, bf16[4,384,384]{2,1,0:T(8,128)(2,1)S(1)} %copy-done.8, ...), custom_call_target="tpu_custom_call", output_to_operand_aliasing={{1}: (6, {})} | custom-call | flops 2000000000 | bytes 1000000 | tf_op jit(solution)/shard_map/pallas_call | solution.py:439
  103.1 33.3 %all_to_all.10.packed = bf16[32,48,384]{2,1,0:T(8,128)(2,1)S(1)} all-to-all(bf16[32,48,384]{2,1,0:T(8,128)(2,1)S(1)} %get-tuple-element.59), channel_id=1, replica_groups=mesh['segment'=8,'dp'=32] {'dp'}, dimensions={0} | all-to-all | bytes 2359296 | tf_op jit(solution)/shard_map/all_to_all | solution.py:446
  136.6 7.9 %collective-permute-start.9 = (f32[24,384]{1,0:T(8,128)S(1)}, f32[24,384]{1,0:T(8,128)S(1)}, u32[]{:S(2)}, u32[]{:S(2)}) collective-permute-start(f32[24,384]{1,0:T(8,128)S(1)} %get-tuple-element.61), channel_id=1, source_target_pairs={{0,32},{32,0},{64,96},{96,64},{128,160},{160,128},{192,224},{224,1... | collective-permute-start | bytes 110600 | tf_op jit(solution)/shard_map/ppermute | solution.py:450
  145.4 1.3 shard_map.114
  (64 shorter events, 12.3 us)
Async XLA Ops:
  0.6 67.9 %copy-start = (bf16[2,1,14,14,384]{4,0,3,2,1:T(2,128)(2,1)S(1)}, bf16[2,1,14,14,384]{4,0,3,2,1:T(2,128)(2,1)}, u32[]{:S(2)}) copy-start(bf16[2,1,14,14,384]{4,0,3,2,1:T(2,128)(2,1)} %param.9) | copy-start | bytes 903172
  0.6 4.2 %collective-permute-start = (s32[1]{0:T(128)}, s32[1]{0:T(128)}, u32[]{:S(2)}, u32[]{:S(2)}) collective-permute-start(s32[1]{0:T(128)} %param.11), channel_id=1, source_target_pairs={{0,32},{32,0},{64,96},{96,64},{128,160},{160,128},{192,224},{224,1... | collective-permute-start | bytes 20 | tf_op jit(solution)/shard_map/ppermute | solution.py:370
  8.8 1.3 collective-permute-start.1
  11.2 9.6 %copy-start.3 = (s32[2,2]{1,0:T(2,128)S(1)}, s32[2,2]{1,0:T(2,128)}, u32[]{:S(2)}) copy-start(s32[2,2]{1,0:T(2,128)} %picks.5) | copy-start | bytes 52
  11.2 9.7 %copy-start.4 = (bf16[2,48,25,384]{3,1,2,0:T(8,128)(2,1)S(1)}, bf16[2,48,25,384]{3,1,2,0:T(8,128)(2,1)}, u32[]{:S(2)}) copy-start(bf16[2,48,25,384]{3,1,2,0:T(8,128)(2,1)} %param.12) | copy-start | bytes 5529604
  11.2 39.2 %all-to-all-start = ((bf16[32,48,384]{2,1,0:T(8,128)(2,1)}), bf16[32,48,384]{2,1,0:T(8,128)(2,1)S(1)}, u32[]{:S(2)}, u32[]{:S(2)}) async-start(bf16[32,48,384]{2,1,0:T(8,128)(2,1)} %shard_map.104), calls=%async_computation | async-start | bytes 2359296 | tf_op jit(solution)/shard_map/all_to_all | solution.py:383
  20.9 1.5 %copy-start.5 = (f32[2,48,12,384]{3,1,2,0:T(8,128)S(1)}, f32[2,48,12,384]{3,1,2,0:T(8,128)}, u32[]{:S(2)}) copy-start(f32[2,48,12,384]{3,1,2,0:T(8,128)} %param.14) | copy-start | bytes 5308420
  23.8 3.0 %copy-start.23 = (bf16[1,14,14,384]{3,2,1,0:T(8,128)(2,1)S(1)}, bf16[1,14,14,384]{3,2,1,0:T(8,128)(2,1)}, u32[]{:S(2)}) copy-start(bf16[1,14,14,384]{3,2,1,0:T(8,128)(2,1)} %param.8) | copy-start | bytes 451588
  26.2 1.5 %collective-permute-start.2 = (bf16[2,25,384]{2,1,0:T(8,128)(2,1)S(1)}, bf16[2,25,384]{2,1,0:T(8,128)(2,1)S(1)}, u32[]{:S(2)}, u32[]{:S(2)}) collective-permute-start(bf16[2,25,384]{2,1,0:T(8,128)(2,1)S(1)} %get-tuple-element.39), channel_id=1, source_target_pairs={{0,32},{32,0},{64,96},{96,64},{128,160},{160,128},{192,224},{224,1... | collective-permute-start | bytes 115208 | tf_op jit(solution)/shard_map/ppermute | solution.py:397
  54.9 11.7 %copy-start.7 = (bf16[4,384,384]{2,1,0:T(8,128)(2,1)}, bf16[4,384,384]{2,1,0:T(8,128)(2,1)S(1)}, u32[]{:S(2)}) copy-start(bf16[4,384,384]{2,1,0:T(8,128)(2,1)S(1)} %get-tuple-element.41.wall) | copy-start | bytes 3538948
  54.9 5.5 %collective-permute-start.3 = (bf16[224,384]{1,0:T(8,128)(2,1)S(1)}, bf16[224,384]{1,0:T(8,128)(2,1)S(1)}, u32[]{:S(2)}, u32[]{:S(2)}) collective-permute-start(bf16[224,384]{1,0:T(8,128)(2,1)S(1)} %get-tuple-element.40), channel_id=1, source_target_pairs={{0,64},{32,96},{64,128},{96,160},{128,192},{160,224},{192,0},{224,... | collective-permute-start | bytes 516104 | tf_op jit(solution)/shard_map/ppermute | solution.py:412
  61.0 5.5 %collective-permute-start.4 = (bf16[224,384]{1,0:T(8,128)(2,1)S(1)}, bf16[224,384]{1,0:T(8,128)(2,1)S(1)}, u32[]{:S(2)}, u32[]{:S(2)}) collective-permute-start(bf16[224,384]{1,0:T(8,128)(2,1)S(1)} %get-tuple-element.45), channel_id=1, source_target_pairs={{0,64},{32,96},{64,128},{96,160},{128,192},{160,224},{192,0},{224,... | collective-permute-start | bytes 516104 | tf_op jit(solution)/shard_map/ppermute | solution.py:421
  68.0 5.5 %collective-permute-start.5 = (bf16[224,384]{1,0:T(8,128)(2,1)S(1)}, bf16[224,384]{1,0:T(8,128)(2,1)S(1)}, u32[]{:S(2)}, u32[]{:S(2)}) collective-permute-start(bf16[224,384]{1,0:T(8,128)(2,1)S(1)} %get-tuple-element.48), channel_id=1, source_target_pairs={{0,64},{32,96},{64,128},{96,160},{128,192},{160,224},{192,0},{224,... | collective-permute-start | bytes 516104 | tf_op jit(solution)/shard_map/ppermute | solution.py:421
  68.5 5.0 %copy-start.8 = (bf16[4,384,384]{2,1,0:T(8,128)(2,1)S(1)}, bf16[4,384,384]{2,1,0:T(8,128)(2,1)}, u32[]{:S(2)}) copy-start(bf16[4,384,384]{2,1,0:T(8,128)(2,1)} %copy-done.7) | copy-start | bytes 3538948
  75.1 10.3 %copy-start.11 = (bf16[4,224,384]{2,1,0:T(8,128)(2,1)}, bf16[4,224,384]{2,1,0:T(8,128)(2,1)S(1)}, u32[]{:S(2)}) copy-start(bf16[4,224,384]{2,1,0:T(8,128)(2,1)S(1)} %get-tuple-element.57.hs) | copy-start | bytes 2064388
  75.1 9.6 %collective-permute-start.6 = (bf16[224,384]{1,0:T(8,128)(2,1)S(1)}, bf16[224,384]{1,0:T(8,128)(2,1)S(1)}, u32[]{:S(2)}, u32[]{:S(2)}) collective-permute-start(bf16[224,384]{1,0:T(8,128)(2,1)S(1)} %get-tuple-element.51), channel_id=1, source_target_pairs={{0,192},{32,224},{64,0},{96,32},{128,64},{160,96},{192,128},{224,1... | collective-permute-start | bytes 516104 | tf_op jit(solution)/shard_map/ppermute | solution.py:429
  85.4 6.3 %collective-permute-start.7 = (bf16[224,384]{1,0:T(8,128)(2,1)S(1)}, bf16[224,384]{1,0:T(8,128)(2,1)S(1)}, u32[]{:S(2)}, u32[]{:S(2)}) collective-permute-start(bf16[224,384]{1,0:T(8,128)(2,1)S(1)} %get-tuple-element.54), channel_id=1, source_target_pairs={{0,192},{32,224},{64,0},{96,32},{128,64},{160,96},{192,128},{224,1... | collective-permute-start | bytes 516104 | tf_op jit(solution)/shard_map/ppermute | solution.py:438
  91.8 7.7 %copy-start.12 = (bf16[4,224,384]{2,1,0:T(8,128)(2,1)S(1)}, bf16[4,224,384]{2,1,0:T(8,128)(2,1)}, u32[]{:S(2)}) copy-start(bf16[4,224,384]{2,1,0:T(8,128)(2,1)} %copy-done.11) | copy-start | bytes 2064388
  92.3 7.1 %collective-permute-start.8 = (bf16[224,384]{1,0:T(8,128)(2,1)S(1)}, bf16[224,384]{1,0:T(8,128)(2,1)S(1)}, u32[]{:S(2)}, u32[]{:S(2)}) collective-permute-start(bf16[224,384]{1,0:T(8,128)(2,1)S(1)} %get-tuple-element.56), channel_id=1, source_target_pairs={{0,192},{32,224},{64,0},{96,32},{128,64},{160,96},{192,128},{224,1... | collective-permute-start | bytes 516104 | tf_op jit(solution)/shard_map/ppermute | solution.py:438
  136.4 9.0 %copy-start.16 = (f32[24,384]{1,0:T(8,128)S(1)}, f32[24,384]{1,0:T(8,128)}, u32[]{:S(2)}) copy-start(f32[24,384]{1,0:T(8,128)} %copy-done.15) | copy-start | bytes 110596
  136.5 9.0 %copy-start.18 = (f32[24,384]{1,0:T(8,128)S(1)}, f32[24,384]{1,0:T(8,128)}, u32[]{:S(2)}) copy-start(f32[24,384]{1,0:T(8,128)} %copy-done.17) | copy-start | bytes 110596
  136.5 9.0 %copy-start.20 = (f32[24,384]{1,0:T(8,128)S(1)}, f32[24,384]{1,0:T(8,128)}, u32[]{:S(2)}) copy-start(f32[24,384]{1,0:T(8,128)} %copy-done.19) | copy-start | bytes 110596
  136.5 9.0 %copy-start.22 = (f32[24,384]{1,0:T(8,128)S(1)}, f32[24,384]{1,0:T(8,128)}, u32[]{:S(2)}) copy-start(f32[24,384]{1,0:T(8,128)} %copy-done.21) | copy-start | bytes 110596
  136.6 8.8 %collective-permute-start.9 = (f32[24,384]{1,0:T(8,128)S(1)}, f32[24,384]{1,0:T(8,128)S(1)}, u32[]{:S(2)}, u32[]{:S(2)}) collective-permute-start(f32[24,384]{1,0:T(8,128)S(1)} %get-tuple-element.61), channel_id=1, source_target_pairs={{0,32},{32,0},{64,96},{96,64},{128,160},{160,128},{192,224},{224,1... | collective-permute-start | bytes 110600 | tf_op jit(solution)/shard_map/ppermute | solution.py:450
  (11 other events, 9.2 us)
